TPU v7x, 32 devices: a whole 2x2x4 slice. The times are simulated.
32 devices in a mesh: narrow: 4 (over y, core), wide: 8 (over z, x).
Axes of the slice: x: 2, y: 2, z: 4, core: 2. Of those that a mesh axis runs over, the one named last changes fastest.
Arguments:
- normed: bfloat16 [1024, 2048], P('wide', 'narrow'), may hold values from -6 to 6
- router_weight: bfloat16 [2048, 128], P('narrow'), may hold values from -0.125 to 0.125
- gate_up_weight: bfloat16 [128, 2, 2048, 768], P('wide', None, 'narrow'), may hold values from -0.1875 to 0.1875
- down_weight: bfloat16 [128, 768, 2048], P('wide', 'narrow'), may hold values from -0.3125 to 0.3125
- expert_ids: int32 [1024, 8], P('wide'), may hold values from 0 to 127, all different within a row; in each aligned block of 128 rows (0 to 127, 128 to 255, ...) at most 16 rows name the same one
Outputs:
- mixed: bfloat16 [1024, 2048], P('wide', 'narrow')
Inputs may be any that keep to these rules, and one draw needn't show every extreme that they name: `expert_ids`: each row names 8 different experts. In each aligned block of 128 rows (the rows of one index of wide) no expert is named by more than 16 rows, and in every draw some expert is named by exactly 16 rows of some block.
All inputs are finite; a program needn't handle non-finite values.
Results may differ from a plain program's by a relative error of at most 0.023.
Values may be sent and summed in bfloat16 or wider, within the bound.
No kernel may reach another device: no remote copies, remote signals or barrier semaphores. Data moves between devices by JAX's collectives and lax.ppermute only.
A program may use at most 128 MiB of HBM per device.

v0:
```python
import jax
import jax.numpy as jnp
from jax import lax
from jax.sharding import PartitionSpec as P

TOPK = 8
CAP = 16


def local(normed, router_weight, gate_up_weight, down_weight, expert_ids):
    tok_count = normed.shape[0]
    share_width = normed.shape[1]
    experts = router_weight.shape[1]
    local_experts = gate_up_weight.shape[0]
    capacity = CAP
    blocks = lax.axis_size("wide")
    pair_count = tok_count * TOPK
    logits = lax.psum(
        jnp.dot(normed, router_weight, preferred_element_type=jnp.float32).astype(jnp.bfloat16),
        "narrow",
    ).astype(jnp.float32)
    picker = (expert_ids[:, :, None] == jnp.arange(experts, dtype=jnp.int32)[None, None, :]).astype(
        jnp.float32
    )
    chosen = jnp.sum(picker * logits[:, None, :], axis=2)
    scores = jnp.exp(chosen)
    weights = scores / jnp.sum(scores, axis=1, keepdims=True)
    pair_ids = expert_ids.reshape(-1)
    onehot = (pair_ids[:, None] == jnp.arange(experts, dtype=jnp.int32)[None, :]).astype(jnp.int32)
    running = jnp.cumsum(onehot, axis=0) - onehot
    order_in = jnp.sum(running * onehot, axis=1)
    owner = pair_ids // local_experts
    local_of_pair = pair_ids - owner * local_experts
    out_index = (local_of_pair * blocks + owner) * capacity + order_in
    token_in_block = jnp.arange(pair_count, dtype=jnp.int32) // TOPK
    slot_total = local_experts * blocks * capacity
    gathered, all_ids = (
        lax.all_gather(normed, "wide", axis=0, tiled=True),
        lax.all_gather(expert_ids.astype(jnp.bfloat16), "wide", axis=0, tiled=True),
    )
    all_ids = all_ids.astype(jnp.int32).reshape(blocks, pair_count)
    first_expert = lax.axis_index("wide") * local_experts
    local_ids = all_ids - first_expert
    local_hot = (
        local_ids[:, :, None] == jnp.arange(local_experts, dtype=jnp.int32)[None, None, :]
    ).astype(jnp.int32)
    local_running = jnp.cumsum(local_hot, axis=1) - local_hot
    order_all = jnp.sum(local_running * local_hot, axis=2)
    block_index = jnp.arange(blocks, dtype=jnp.int32)[:, None]
    is_mine = (local_ids >= 0) & (local_ids < local_experts)
    destination = jnp.where(
        is_mine, (local_ids * blocks + block_index) * capacity + order_all, slot_total
    )
    source_token = block_index * tok_count + token_in_block[None, :]
    slot_table = (
        jnp.full((slot_total,), blocks * tok_count, jnp.int32)
        .at[destination.reshape(-1)]
        .set(source_token.reshape(-1), mode="drop")
    )
    padded = jnp.concatenate([gathered, jnp.zeros((1, share_width), gathered.dtype)], axis=0)
    arrived = padded[slot_table].reshape(local_experts, blocks, capacity, share_width)
    slot_rows = arrived.reshape(local_experts, blocks * capacity, share_width)
    gate_terms = jnp.einsum(
        "erd,edf->erf", slot_rows, gate_up_weight[:, 0], preferred_element_type=jnp.float32
    )
    up_terms = jnp.einsum(
        "erd,edf->erf", slot_rows, gate_up_weight[:, 1], preferred_element_type=jnp.float32
    )
    gate_sum, up_sum = (
        lax.psum_scatter(
            gate_terms.astype(jnp.bfloat16), "narrow", scatter_dimension=2, tiled=True
        ).astype(jnp.float32),
        lax.psum_scatter(
            up_terms.astype(jnp.bfloat16), "narrow", scatter_dimension=2, tiled=True
        ).astype(jnp.float32),
    )
    hidden = (jax.nn.silu(gate_sum) * up_sum).astype(jnp.bfloat16)
    expert_terms = jnp.einsum(
        "erf,efd->erd", hidden, down_weight, preferred_element_type=jnp.float32
    )
    expert_out = lax.psum_scatter(
        expert_terms.astype(jnp.bfloat16), "narrow", scatter_dimension=2, tiled=True
    )
    expert_out = expert_out.reshape(local_experts, blocks, capacity, share_width)
    returned = lax.all_to_all(expert_out, "wide", split_axis=1, concat_axis=1, tiled=True)
    flat_out = returned.reshape(slot_total, share_width)
    picked = flat_out[out_index].reshape(tok_count, TOPK, share_width)
    combined = jnp.sum(weights[:, :, None] * picked.astype(jnp.float32), axis=1)
    return combined.astype(jnp.bfloat16)


def solution(mesh):
    placed = (
        P("wide", "narrow"),
        P("narrow", None),
        P("wide", None, "narrow", None),
        P("wide", "narrow", None),
        P("wide", None),
    )
    return jax.shard_map(
        local, mesh=mesh, in_specs=placed, out_specs=P("wide", "narrow"), check_vma=False
    )
```

profile of v0, /device:TPU:0, one launch (start us, length us, event | category | flops | bytes accessed | tf_op | source)
XLA Modules:
  0.0 355.1 jit_solution(15422865398020943970)
XLA Ops:
  6.5 0.7 all-gather.2.cloned.1.call-update
  7.3 0.7 convert_element_type.56
  8.0 27.9 %all_gather.7 = bf16[1024,8]{0,1:T(8,128)(2,1)S(1)} all-gather(bf16[128,8]{0,1:T(8,128)(2,1)S(1)} %convert_element_type.56), channel_id=1, replica_groups=mesh['narrow'=4,'wide'=8] {'wide'}, dimensions={0}, use_global_device_ids=true | all-gather | bytes 18432 | tf_op jit(solution)/shard_map/all_gather | solution.py:39
  36.0 0.2 copy.40
  36.2 0.3 sub.55
  36.4 0.3 sub.54
  36.8 36.0 %reduce-window.14 = s32[8,16,8,128]{3,2,1,0:T(8,128)S(1)} reduce-window(s32[8,16,8,128]{3,2,1,0:T(8,128)S(1)} %fusion.26, s32[]{:T(128)} %constant.58.clone.1), window={size=1x1x1x128 pad=0_0x0_0x0_0x127_0}, to_apply=%region_3.0 | reduce-window | flops 16646144 | bytes 1048580 | tf_op jit(solution)/shard_map/reduce-window
  72.8 0.2 slice.28
  73.0 0.5 copy.42
  73.5 0.1 copy.43
  73.6 0.2 broadcast_add_fusion.1
  73.8 0.1 reduce_window_sum.31
  73.9 0.1 fusion.23
  74.1 0.2 copy.39
  74.3 0.3 mul.105
  74.6 0.3 copy.38
  74.9 0.3 and.47
  75.2 0.1 add_bitcast_fusion
  75.3 0.1 compare_select_fusion
  75.4 30.4 %scatter_custom_fusion = s32[2048]{0:T(1024)S(1)} fusion(s32[8192]{0:T(1024)S(1)} %bitcast.67, s32[8192]{0:T(1024)S(1)} %bitcast.68, s32[]{:T(128)} %constant.55.clone.1), kind=kCustom, calls=%fused_computation.64 | custom fusion | bytes 8196 | tf_op jit(solution)/shard_map/scatter | solution.py:58
  105.9 1.3 concatenate.3
  107.2 7.5 %gather_fusion = bf16[2048,512]{1,0:T(8,128)(2,1)S(1)} fusion(bf16[1025,512]{1,0:T(8,128)(2,1)S(1)} %concatenate.3, s32[2048]{0:T(1024)S(1)} %fusion.28), kind=kCustom, calls=%fused_computation | custom fusion | bytes 4202496 | tf_op jit(solution)/shard_map/gather | solution.py:61
  114.7 9.9 %fusion.6 = bf16[16,128,768]{1,2,0:T(8,128)(2,1)} fusion(bf16[16,128,512]{2,1,0:T(8,128)(2,1)S(1)} %bitcast.60, bf16[16,2,512,768]{3,2,1,0:T(8,128)(2,1)} %param.7), kind=kOutput, calls=%fused_computation.10 | convolution fusion | flops 1612185600 | bytes 17825792 | tf_op jit(solution)/shard_map/erd,edf->erf/dot_general | solution.py:63
  124.7 0.2 reduce-scatter.6.cloned.1.call-start
  124.9 10.0 %fusion.9 = bf16[16,128,768]{1,2,0:T(8,128)(2,1)} fusion(bf16[16,128,512]{2,1,0:T(8,128)(2,1)S(1)} %bitcast.61, bf16[16,2,512,768]{3,2,1,0:T(8,128)(2,1)} %param.7), kind=kOutput, calls=%fused_computation.11 | convolution fusion | flops 1612185600 | bytes 17825792 | tf_op jit(solution)/shard_map/erd,edf->erf/dot_general | solution.py:66
  134.9 27.1 %reduce-scatter.4.cloned.1.call-done = bf16[16,128,192]{1,2,0:T(8,128)(2,1)} async-done(((bf16[16,128,768]{1,2,0:T(8,128)(2,1)}), bf16[16,128,192]{1,2,0:T(8,128)(2,1)}) %reduce-scatter.4.cloned.1.call-update) | async-done | bytes 786448 | tf_op jit(solution)/shard_map/reduce_scatter | solution.py:70
  162.0 40.3 %reduce-scatter.6.cloned.1.call-done = bf16[16,128,192]{1,2,0:T(8,128)(2,1)} async-done(((bf16[16,128,768]{1,2,0:T(8,128)(2,1)}), bf16[16,128,192]{1,2,0:T(8,128)(2,1)}) %reduce-scatter.6.cloned.1.call-update) | async-done | bytes 786448 | tf_op jit(solution)/shard_map/reduce_scatter | solution.py:73
  202.4 10.7 %convolution_convert_fusion = bf16[16,128,2048]{2,1,0:T(8,128)(2,1)} fusion(bf16[16,192,2048]{2,1,0:T(8,128)(2,1)} %param.8, bf16[16,128,192]{1,2,0:T(8,128)(2,1)} %reduce-scatter.6.cloned.1.call-done, bf16[16,128,192]{1,2,0:T(8,128)(2,1)} %reduce-scatter.4.cloned.1.call-done), kind=kOutput, calls=%fused_computation.9 | convolution fusion | flops 1617952768 | bytes 22544384 | tf_op jit(solution)/shard_map/erf,efd->erd/dot_general | solution.py:78
  213.1 71.4 %reduce-scatter.8.cloned.1.call-done = bf16[16,128,512]{2,1,0:T(8,128)(2,1)} async-done(((bf16[16,128,2048]{2,1,0:T(8,128)(2,1)}), bf16[16,128,512]{2,1,0:T(8,128)(2,1)}) %reduce-scatter.8.cloned.1.call-update) | async-done | bytes 2097168 | tf_op jit(solution)/shard_map/reduce_scatter | solution.py:81
  284.5 3.2 copy.46
  287.6 5.6 %all-to-all-start = ((bf16[16,8,16,512]{3,2,0,1:T(8,128)(2,1)}), bf16[16,8,16,512]{3,2,0,1:T(8,128)(2,1)}, u32[]{:S(2)}, u32[]{:S(2)}) async-start(bf16[16,8,16,512]{3,2,0,1:T(8,128)(2,1)} %copy.46), calls=%async_computation.3 | async-start | bytes 4194304 | tf_op jit(solution)/shard_map/all_to_all | solution.py:85
  293.3 0.1 copy.37
  293.4 0.1 eq.72
  293.5 0.1 eq.68
  293.6 0.1 reshape.275
  293.7 0.1 copy.51
  293.8 0.2 fusion.24
  294.1 0.1 copy.52
  294.2 0.2 convolution_convert_fusion.1
  294.4 11.1 %psum.7 = bf16[128,128]{1,0:T(8,128)(2,1)S(1)} all-reduce(bf16[128,128]{1,0:T(8,128)(2,1)S(1)} %convolution_convert_fusion.1), channel_id=1, replica_groups=mesh['narrow'=4,'wide'=8] {'narrow'}, use_global_device_ids=true, to_apply=%region_0.0 | all-reduce | flops 16384 | bytes 65536 | tf_op jit(solution)/shard_map/psum | solution.py:18
  305.5 0.4 select_reduce_fusion
  305.8 0.1 exponential_reduce_fusion
  306.0 0.4 fusion.21
  306.4 0.1 exponential_divide_fusion
  306.5 35.0 %all-to-all-done = bf16[16,8,16,512]{3,2,0,1:T(8,128)(2,1)} async-done(((bf16[16,8,16,512]{3,2,0,1:T(8,128)(2,1)}), bf16[16,8,16,512]{3,2,0,1:T(8,128)(2,1)}, u32[]{:S(2)}, u32[]{:S(2)}) %all-to-all-start) | async-done | bytes 2097184 | tf_op jit(solution)/shard_map/all_to_all | solution.py:85
  341.5 1.8 copy.47
  343.2 4.0 %gather_fusion.1 = bf16[1024,512]{1,0:T(8,128)(2,1)S(1)} fusion(bf16[2048,512]{1,0:T(8,128)(2,1)S(1)} %bitcast.59, s32[1024]{0:T(1024)S(1)} %broadcast_clamp_fusion), kind=kCustom, calls=%fused_computation.1 | custom fusion | bytes 2101248 | tf_op jit(solution)/shard_map/gather | solution.py:87
  347.2 1.4 fusion.12
  (32 shorter events, 0.5 us)
Async XLA Ops:
  6.5 287.7 %copy-start = (bf16[512,128]{1,0:T(8,128)(2,1)S(1)}, bf16[512,128]{1,0:T(8,128)(2,1)}, u32[]{:S(2)}) copy-start(bf16[512,128]{1,0:T(8,128)(2,1)} %param.6) | copy-start | bytes 393220
  6.5 99.3 %all-gather.2.cloned.1.call-start = ((), (), s32[]{:S(2)}) async-start(), calls=%async_computation.4 | async-start | bytes 1179648 | tf_op jit(solution)/shard_map/all_gather | solution.py:38
  7.3 154.8 %reduce-scatter.4.cloned.1.call-start = ((), (), s32[]{:S(2)}) async-start(), calls=%async_computation.5 | async-start | bytes 3932160 | tf_op jit(solution)/shard_map/reduce_scatter | solution.py:70
  124.7 77.7 %reduce-scatter.6.cloned.1.call-start = ((), (), s32[]{:S(2)}) async-start(), calls=%async_computation.6 | async-start | bytes 3932160 | tf_op jit(solution)/shard_map/reduce_scatter | solution.py:73
  134.9 149.6 %reduce-scatter.8.cloned.1.call-start = ((), (), s32[]{:S(2)}) async-start(), calls=%async_computation.7 | async-start | bytes 10485760 | tf_op jit(solution)/shard_map/reduce_scatter | solution.py:81
  287.6 5.6 %copy-start.2 = (s32[128,8]{0,1:T(8,128)S(1)}, s32[128,8]{0,1:T(8,128)}, u32[]{:S(2)}) copy-start(s32[128,8]{0,1:T(8,128)} %param.9) | copy-start | bytes 12292
  287.6 53.8 %all-to-all-start = ((bf16[16,8,16,512]{3,2,0,1:T(8,128)(2,1)}), bf16[16,8,16,512]{3,2,0,1:T(8,128)(2,1)}, u32[]{:S(2)}, u32[]{:S(2)}) async-start(bf16[16,8,16,512]{3,2,0,1:T(8,128)(2,1)} %copy.46), calls=%async_computation.3 | async-start | bytes 4194304 | tf_op jit(solution)/shard_map/all_to_all | solution.py:85
  293.3 0.9 copy-start.1
Sparse Core Ops, SparseCore 0:
  9.5 42.9 all-gather.1
  124.8 37.1 reduce-scatter.3
  164.6 37.7 reduce-scatter.5
  213.2 71.2 reduce-scatter.7
where the time goes:
time: 356 us; the launch traced here: 355 us
  waiting for transfers between devices  175 us (49%)
  local copies, waits for them, and re-layouts  51.5 us (14%)
  other arithmetic  40 us (11%)
  blocking collectives  39 us (11%)
  matrix products  30.7 us (9%)
  between operations  13.4 us (4%)
  starting transfers between devices  5.94 us (2%)
    reduce_scatter x1, waiting for transfers between devices, local(): lax.psum_scatter(expert_terms.astype(jnp.bfloat16), 'narrow', scatter_dim...  71.4 us
    reduce_scatter x1, waiting for transfers between devices, local(): lax.psum_scatter(up_terms.astype(jnp.bfloat16), 'narrow', scatter_dimensi...  40.3 us
    another operation x6, other arithmetic  36.5 us
    all_to_all x1, waiting for transfers between devices, local(): lax.all_to_all(expert_out, 'wide', split_axis=1, concat_axis=1, tiled=True)  35 us
    scatter x1, local copies, waits for them, and re-layouts, local(): slot_table = jnp.full((slot_total,), blocks * tok_count, jnp.int32).at[de...  30.4 us
    all_gather x1, blocking collectives, local(): lax.all_gather(expert_ids.astype(jnp.bfloat16), 'wide', axis=0, tiled=True)  27.9 us
    reduce_scatter x1, waiting for transfers between devices, local(): lax.psum_scatter(gate_terms.astype(jnp.bfloat16), 'narrow', scatter_dimen...  27.1 us
    psum x1, blocking collectives, local(): lax.psum(jnp.dot(normed, router_weight, preferred_element_type=jnp.float3...  11.1 us
  transfers between devices with their start and end apart: 5, of which 4 were waited for; matrix products, arithmetic and copies ran while one was open for 23% of the time, Pallas kernels for 0%

commit v1 on v0

v1 whole, which is shorter than its diff:
```python
import functools

import jax
import jax.numpy as jnp
from jax import lax
from jax.experimental import pallas as pl
from jax.experimental.pallas import tpu as pltpu
from jax.sharding import PartitionSpec as P


TOPK = 8
CAP = 16
GROUP = 4
TILE = GROUP * CAP
ALIGN = 16
F32 = jnp.float32
BF16 = jnp.bfloat16


def swap(x, axis, mask):
    size = lax.axis_size(axis)
    return lax.ppermute(x, axis, [(i, i ^ mask) for i in range(size)])


def gate_up_kernel(place, ids, tokens, router, weight, near, far, send, pos, meta, buffer, arrived, *,
                   blocks, local_experts):
    total = tokens.shape[0]
    tok = total // blocks
    copies = [pltpu.make_async_copy(weight.at[e], buffer.at[e], arrived.at[e]) for e in range(local_experts)]
    for copy in copies:
        copy.start()

    lane = lax.broadcasted_iota(jnp.int32, (tok, tok), 0)
    before = (lane < lax.broadcasted_iota(jnp.int32, (tok, tok), 1)).astype(BF16)
    expert = lax.broadcasted_iota(jnp.int32, (max(local_experts, 8), tok), 0) + place[1]
    every = lax.broadcasted_iota(jnp.int32, (router.shape[1], tok), 0)
    offset = jnp.zeros((max(local_experts, 8), 1), F32)
    ranks, hots, chosen = [], [], []
    for b in range(blocks):
        hot = jnp.zeros(expert.shape, F32)
        logits = jnp.dot(tokens[b * tok:(b + 1) * tok, :], router[...], preferred_element_type=F32).T
        for k in range(TOPK):
            row = ids[b * TOPK + k:b * TOPK + k + 1, :]
            hot = jnp.where(row == expert, 1.0, hot)
            chosen.append(jnp.sum(jnp.where(row == every, logits, 0.0), axis=0, keepdims=True))
        ranks.append(jnp.dot(hot.astype(BF16), before, preferred_element_type=F32) + offset)
        hots.append(hot)
        offset = offset + jnp.sum(hot, axis=1, keepdims=True)
    slots = local_experts * TILE
    extra = jnp.concatenate(
        [jnp.concatenate(chosen[2 * TOPK * p:2 * TOPK * (p + 1)], axis=0) for p in range(blocks // 2)]
        + [jnp.zeros((2 * TOPK, near.shape[1] - tok * (blocks // 2)), F32)], axis=1).astype(BF16)
    near[slots:, :] = extra
    far[slots:, :] = extra
    send[0, slots:, :] = extra
    send[1, slots:, :] = extra

    rank = jnp.concatenate(ranks, axis=1).astype(jnp.int32)
    hot = jnp.concatenate(hots, axis=1)
    mine = place[0]
    flip_core = (mine & 1) == 1
    flip_chip = (mine & 2) == 2
    slot = lax.broadcasted_iota(jnp.int32, (TILE, total), 0)
    start = jnp.int32(0)
    for e in range(local_experts):
        count = jnp.sum(offset[e:e + 1, :]).astype(jnp.int32)
        at = jnp.where(hot[e:e + 1] > 0.0, rank[e:e + 1], -1)
        pos[e:e + 1, :] = at
        meta[e] = start
        start = pl.multiple_of(start, ALIGN)
        pick = (slot == at).astype(F32).astype(BF16)
        x = jnp.dot(pick, tokens[...], preferred_element_type=F32).astype(BF16)
        copies[e].wait()
        g = jnp.dot(x, buffer[e, 0], preferred_element_type=F32)
        u = jnp.dot(x, buffer[e, 1], preferred_element_type=F32)
        quarter = g.shape[1] // 4
        d = [jnp.concatenate([g[:, q * quarter:(q + 1) * quarter], u[:, q * quarter:(q + 1) * quarter]], axis=1)
             for q in range(4)]
        d = [jnp.where(flip_core, d[q ^ 1], d[q]) for q in range(4)]
        d = [jnp.where(flip_chip, d[q ^ 2], d[q]).astype(BF16) for q in range(4)]
        near[pl.ds(start, TILE), :] = d[0]
        send[0, pl.ds(start, TILE), :] = d[1]
        far[pl.ds(start, TILE), :] = d[2]
        send[1, pl.ds(start, TILE), :] = d[3]
        start = start + (count + ALIGN - 1) // ALIGN * ALIGN


VMEM = pl.BlockSpec(memory_space=pltpu.VMEM)
SMEM = pl.BlockSpec(memory_space=pltpu.SMEM)
HBM = pl.BlockSpec(memory_space=pltpu.HBM)


def gate_up(place, ids, tokens, router, weight, blocks):
    total, width = tokens.shape
    local_experts, _, _, units = weight.shape
    half = units // 2
    rows = local_experts * TILE + 2 * TOPK
    return pl.pallas_call(
        functools.partial(gate_up_kernel, blocks=blocks, local_experts=local_experts),
        in_specs=[SMEM, VMEM, VMEM, VMEM, HBM],
        out_specs=[VMEM, VMEM, VMEM, VMEM, SMEM],
        scratch_shapes=[pltpu.VMEM(weight.shape, BF16), pltpu.SemaphoreType.DMA((local_experts,))],
        out_shape=[jax.ShapeDtypeStruct((rows, half), BF16), jax.ShapeDtypeStruct((rows, half), BF16),
                   jax.ShapeDtypeStruct((2, rows, half), BF16),
                   jax.ShapeDtypeStruct((max(local_experts, 8), total), jnp.int32),
                   jax.ShapeDtypeStruct((max(local_experts, 8),), jnp.int32)],
        compiler_params=pltpu.CompilerParams(vmem_limit_bytes=36 * 1024 * 1024),
        cost_estimate=pl.CostEstimate(flops=6 * rows * width * units, bytes_accessed=2 * weight.size,
                                      transcendentals=0),
        name="gate_up",
    )(place, ids, tokens, router, weight)


def down_kernel(place, meta, ids, pos, near, beside, across, weight, keep, far, send,
                terms, picks, picks_t, buffer, arrived, *, blocks, local_experts):
    total, width = keep.shape
    tok = total // blocks
    cap = local_experts * TILE
    copies = [pltpu.make_async_copy(weight.at[e], buffer.at[e], arrived.at[e]) for e in range(local_experts)]
    for copy in copies:
        copy.start()

    expert = lax.broadcasted_iota(jnp.int32, (max(local_experts, 8), tok), 0) + place[1]
    extra = near[cap:, :].astype(F32) + beside[0, cap:, :].astype(F32) + across[cap:, :].astype(F32)
    values = []
    for b in range(blocks):
        scores = jnp.exp(extra[b % 2 * TOPK:(b % 2 + 1) * TOPK, b // 2 * tok:(b // 2 + 1) * tok])
        scores = scores / jnp.sum(scores, axis=0, keepdims=True)
        value = jnp.zeros(expert.shape, F32)
        for k in range(TOPK):
            row = ids[b * TOPK + k:b * TOPK + k + 1, :]
            value = jnp.where(row == expert, scores[k:k + 1, :], value)
        values.append(value)
    share = jnp.concatenate(values, axis=1)

    def clear(j, carry):
        start = pl.multiple_of(j * TILE, TILE)
        for q in range(4):
            terms[q, pl.ds(start, TILE), :] = jnp.zeros((TILE, width), BF16)
        picks[pl.ds(start, TILE), :] = jnp.zeros((TILE, total), BF16)
        return carry

    lax.fori_loop(meta[local_experts - 1] // TILE, cap // TILE, clear, 0)
    slot = lax.broadcasted_iota(jnp.int32, (TILE, total), 0)
    for e in range(local_experts):
        start = pl.multiple_of(meta[e], ALIGN)
        pick = slot == pos[e:e + 1, :]
        picks[pl.ds(start, TILE), :] = pick.astype(F32).astype(BF16)
        scale = jnp.sum(jnp.where(pick, share[e:e + 1], 0.0), axis=1, keepdims=True)
        s = (near[pl.ds(start, TILE), :].astype(F32) + beside[0, pl.ds(start, TILE), :].astype(F32)
             + across[pl.ds(start, TILE), :].astype(F32))
        half = s.shape[1] // 2
        g = s[:, :half]
        h = (g / (1.0 + jnp.exp(-g)) * s[:, half:] * scale).astype(BF16)
        copies[e].wait()
        t = jnp.dot(h, buffer[e], preferred_element_type=F32).astype(BF16)
        for q in range(4):
            terms[q, pl.ds(start, TILE), :] = t[:, q * width:(q + 1) * width]

    mine = place[0]
    picks_t[...] = picks[...].T
    send[0] = jnp.dot(picks_t[...], terms[mine ^ 1], preferred_element_type=F32).astype(BF16)
    send[1] = jnp.dot(picks_t[...], terms[mine ^ 3], preferred_element_type=F32).astype(BF16)
    far[...] = jnp.dot(picks_t[...], terms[mine ^ 2], preferred_element_type=F32).astype(BF16)
    keep[...] = jnp.dot(picks_t[...], terms[mine], preferred_element_type=F32).astype(BF16)


def down(place, meta, ids, pos, near, beside, across, weight, blocks, tok, width):
    local_experts = weight.shape[0]
    cap = local_experts * TILE
    total = blocks * tok
    return pl.pallas_call(
        functools.partial(down_kernel, blocks=blocks, local_experts=local_experts),
        in_specs=[SMEM, SMEM] + [VMEM] * 5 + [HBM],
        out_specs=[VMEM, VMEM, VMEM],
        scratch_shapes=[pltpu.VMEM((4, cap, width), BF16), pltpu.VMEM((cap, total), BF16),
                        pltpu.VMEM((total, cap), BF16), pltpu.VMEM(weight.shape, BF16),
                        pltpu.SemaphoreType.DMA((local_experts,))],
        out_shape=[jax.ShapeDtypeStruct((total, width), BF16), jax.ShapeDtypeStruct((total, width), BF16),
                   jax.ShapeDtypeStruct((2, total, width), BF16)],
        compiler_params=pltpu.CompilerParams(vmem_limit_bytes=36 * 1024 * 1024),
        cost_estimate=pl.CostEstimate(flops=8 * total * cap * width, bytes_accessed=2 * weight.size,
                                      transcendentals=0),
        name="down",
    )(place, meta, ids, pos, near, beside, across, weight)


def add(*parts):
    total = parts[0].astype(F32)
    for part in parts[1:]:
        total = total + part.astype(F32)
    return total.astype(BF16)


def gather_wide(x, size):
    chunks, order = [x], [[0]]
    bit = size // 2
    while bit:
        moved = [swap(p, "wide", bit) for p in chunks]
        flipped = [[j | bit for j in o] for o in order]
        if len(order[0]) < GROUP:
            chunks, order = [jnp.concatenate([chunks[0], moved[0]], axis=0)], [order[0] + flipped[0]]
        else:
            chunks, order = chunks + moved, order + flipped
        bit //= 2
    return chunks, order


def local(normed, router_weight, gate_up_weight, down_weight, expert_ids):
    tok, width = normed.shape
    local_experts = gate_up_weight.shape[0]
    size = lax.axis_size("wide")
    mine = lax.axis_index("narrow")
    place = jnp.stack([mine, lax.axis_index("wide") * local_experts]).astype(jnp.int32)
    ids, _ = gather_wide(expert_ids.T, size)
    tokens, order = gather_wide(normed, size)

    stage = []
    for c in range(len(order)):
        near, far, send, pos, meta = gate_up(place, ids[c], tokens[c], router_weight, gate_up_weight, GROUP)
        beside = swap(send, "narrow", 1)
        far = add(far, beside[1])
        across = swap(far, "narrow", 2)
        stage.append((near, beside, across, pos, meta))
    terms = []
    for c in range(len(order)):
        near, beside, across, pos, meta = stage[c]
        keep, far, send = down(place, meta, ids[c], pos, near, beside, across, down_weight, GROUP, tok, width)
        beside = swap(send, "narrow", 1)
        far = add(far, beside[1])
        across = swap(far, "narrow", 2)
        whole = add(keep, beside[0], across)
        for i, j in enumerate(order[c]):
            piece = whole[i * tok:(i + 1) * tok]
            terms.append(swap(piece, "wide", j) if j else piece)
    return add(*terms)


def solution(mesh):
    placed = (
        P("wide", "narrow"),
        P("narrow", None),
        P("wide", None, "narrow", None),
        P("wide", "narrow", None),
        P("wide", None),
    )

    return jax.shard_map(local, mesh=mesh, in_specs=placed, out_specs=P("wide", "narrow"), check_vma=False)
```

time: 356 us -> 140 us (0.39)
  waiting for transfers between devices: 175 us -> 62 us
  local copies, waits for them, and re-layouts: 51.5 us -> 10.2 us
  blocking collectives: 39 us -> 0 us
  Pallas kernels: 0 us -> 38 us
  other arithmetic: 40 us -> 4.25 us
  matrix products: 30.7 us -> 0 us
  starting transfers between devices: 5.94 us -> 25.2 us
  between operations: 13.4 us -> 0.18 us
    reduce_scatter x3 -> x0, waiting for transfers between devices: 139 us -> none  [the longest x1 71.4 us: local(): lax.psum_scatter(expert_terms.astype(jnp.bfloat16), 'narrow', scatter_dim...]
    ppermute x0 -> x21, waiting for transfers between devices: none -> 62 us  [swap(): return lax.ppermute(x, axis, [(i, i ^ mask) for i in range(size)])]
    pallas_call x0 -> x4, Pallas kernels: none -> 38 us  [the longest x2 20.7 us: gate_up(): pl.pallas_call(functools.partial(gate_up_kernel, blocks=blocks, local_exp...]
    another operation x6 -> x1, other arithmetic: 36.5 us -> 0.08 us  [local(): jnp.stack([mine, lax.axis_index('wide') * local_experts]).astype(jnp.int32)]
    all_to_all x1 -> x0, waiting for transfers between devices: 35 us -> none  [local(): lax.all_to_all(expert_out, 'wide', split_axis=1, concat_axis=1, tiled=True)]
    dot_general x4 -> x0, matrix products: 30.7 us -> none  [the longest x1 10.7 us: local(): jnp.einsum('erf,efd->erd', hidden, down_weight, preferred_element_type=jn...]
    scatter x1 -> x0, local copies, waits for them, and re-layouts: 30.4 us -> none  [local(): slot_table = jnp.full((slot_total,), blocks * tok_count, jnp.int32).at[de...]
    all_gather x1 -> x0, blocking collectives: 27.9 us -> none  [local(): lax.all_gather(expert_ids.astype(jnp.bfloat16), 'wide', axis=0, tiled=True)]
  transfers between devices with their start and end apart: 5 -> 21, of which waited for: 4 -> 13; matrix products, arithmetic and copies ran while one was open for 23% -> 3% of each run, Pallas kernels for 0% -> 27%
where the time goes in v1:
time: 140 us
  waiting for transfers between devices  62 us (44%)
  Pallas kernels  38 us (27%)
  starting transfers between devices  25.2 us (18%)
  local copies, waits for them, and re-layouts  10.2 us (7%)
  other arithmetic  4.25 us (3%)
    ppermute x21, waiting for transfers between devices, swap(): return lax.ppermute(x, axis, [(i, i ^ mask) for i in range(size)])  62 us
    ppermute x21, starting transfers between devices, swap(): return lax.ppermute(x, axis, [(i, i ^ mask) for i in range(size)])  25.2 us
    pallas_call x2, Pallas kernels, gate_up(): pl.pallas_call(functools.partial(gate_up_kernel, blocks=blocks, local_exp...  20.7 us
    pallas_call x2, Pallas kernels, down(): pl.pallas_call(functools.partial(down_kernel, blocks=blocks, local_expert...  17.2 us
    unnamed x8, local copies, waits for them, and re-layouts  10.1 us
  transfers between devices with their start and end apart: 21, of which 13 were waited for; matrix products, arithmetic and copies ran while one was open for 3% of the time, Pallas kernels for 27%

profile of v1, /device:TPU:0, one launch (start us, length us, event | category | flops | bytes accessed | tf_op | source)
XLA Modules:
  0.0 139.9 jit_solution(16973488065644546210)
XLA Ops:
  0.0 4.1 %collective-permute-start = (s32[8,128]{1,0:T(8,128)}, s32[8,128]{1,0:T(8,128)S(1)}, u32[]{:S(2)}, u32[]{:S(2)}) collective-permute-start(s32[8,128]{1,0:T(8,128)} %bitcast.33), channel_id=1, source_target_pairs={{0,4},{1,5},{2,6},{3,7},{4,0},{5,1},{6,2},{7,3},{8,12},{9,13},{10,... | collective-permute-start | bytes 12296 | tf_op jit(solution)/shard_map/ppermute | solution.py:22
  4.1 0.9 constant_dynamic-update-slice_fusion.2
  5.1 0.8 collective-permute-done
  5.9 0.7 pad_add_fusion.1
  6.6 1.9 %collective-permute-start.1 = (s32[16,128]{1,0:T(8,128)S(1)}, s32[16,128]{1,0:T(8,128)S(1)}, u32[]{:S(2)}, u32[]{:S(2)}) collective-permute-start(s32[16,128]{1,0:T(8,128)S(1)} %pad_add_fusion.1), channel_id=1, source_target_pairs={{0,2},{1,3},{2,0},{3,1},{4,6},{5,7},{6,4},{7,5},{8,10},{9,11},{10,... | collective-permute-start | bytes 24584 | tf_op jit(solution)/shard_map/ppermute | solution.py:22
  8.5 4.5 %collective-permute-done.2 = bf16[128,512]{1,0:T(8,128)(2,1)S(1)} collective-permute-done((bf16[128,512]{1,0:T(8,128)(2,1)}, bf16[128,512]{1,0:T(8,128)(2,1)S(1)}, u32[]{:S(2)}, u32[]{:S(2)}) %collective-permute-start.2) | collective-permute-done | bytes 131104 | tf_op jit(solution)/shard_map/ppermute | solution.py:22
  12.9 0.9 pad_maximum_fusion
  13.9 0.1 collective-permute-start.3
  13.9 0.1 pad_add_fusion.2.place
  14.0 0.7 pad_add_fusion.ids
  14.7 6.4 %collective-permute-done.3 = bf16[256,512]{1,0:T(8,128)(2,1)S(1)} collective-permute-done((bf16[256,512]{1,0:T(8,128)(2,1)S(1)}, bf16[256,512]{1,0:T(8,128)(2,1)S(1)}, u32[]{:S(2)}, u32[]{:S(2)}) %collective-permute-start.3) | collective-permute-done | bytes 262176 | tf_op jit(solution)/shard_map/ppermute | solution.py:22
  21.2 1.6 %collective-permute-start.12 = (bf16[512,512]{1,0:T(8,128)(2,1)S(1)}, bf16[512,512]{1,0:T(8,128)(2,1)S(1)}, u32[]{:S(2)}, u32[]{:S(2)}) collective-permute-start(bf16[512,512]{1,0:T(8,128)(2,1)S(1)} %constant_dynamic-update-slice_fusion.tokens), channel_id=1, source_target_pairs={{0,1},{1,0},{2,3},{3,2},{4,5},{5,4},{6,7},{7,6},{8,9},{9,8},{10,11... | collective-permute-start | bytes 1572872 | tf_op jit(solution)/shard_map/ppermute | solution.py:22
  22.7 10.3 %gate_up.2 = (bf16[1040,384]{1,0:T(8,128)(2,1)S(1)}, bf16[1040,384]{1,0:T(8,128)(2,1)S(1)}, bf16[2,1040,384]{2,1,0:T(8,128)(2,1)S(1)}, s32[16,512]{1,0:T(8,128)S(1)}, s32[16]{0:T(128)S(1)}) custom-call(s32[2]{0:T(128)S(1)} %pad_add_fusion.2.place, s32[32,128]{1,0:T(8,128)S(1)} %pad_add_fusion.ids, ...), custom_call_target="tpu_custom_call" | custom-call | flops 2453667840 | bytes 25165824 | tf_op jit(solution)/shard_map/gate_up/pallas_call | solution.py:98
  33.0 0.1 collective-permute-start.4
  33.1 0.6 collective-permute-start.11
  33.7 3.2 %collective-permute-done.11.ids = s32[32,128]{1,0:T(8,128)S(1)} collective-permute-done((s32[32,128]{1,0:T(8,128)S(1)}, s32[32,128]{1,0:T(8,128)S(1)}, u32[]{:S(2)}, u32[]{:S(2)}) %collective-permute-start.11) | collective-permute-done | bytes 16416 | tf_op jit(solution)/shard_map/ppermute | solution.py:22
  36.9 10.5 %gate_up.3 = (bf16[1040,384]{1,0:T(8,128)(2,1)S(1)}, bf16[1040,384]{1,0:T(8,128)(2,1)S(1)}, bf16[2,1040,384]{2,1,0:T(8,128)(2,1)S(1)}, s32[16,512]{1,0:T(8,128)S(1)}, s32[16]{0:T(128)S(1)}) custom-call(s32[2]{0:T(128)S(1)} %pad_add_fusion.2.place, s32[32,128]{1,0:T(8,128)S(1)} %collective-permute-done.11.ids, ...), custom_call_target="tpu_custom_call" | custom-call | flops 2453667840 | bytes 25165824 | tf_op jit(solution)/shard_map/gate_up/pallas_call | solution.py:98
  47.4 0.1 collective-permute-start.13
  47.5 0.2 fusion.1
  47.7 1.6 %collective-permute-start.5 = (bf16[1040,384]{1,0:T(8,128)(2,1)S(1)}, bf16[1040,384]{1,0:T(8,128)(2,1)S(1)}, u32[]{:S(2)}, u32[]{:S(2)}) collective-permute-start(bf16[1040,384]{1,0:T(8,128)(2,1)S(1)} %fusion.1), channel_id=1, source_target_pairs={{0,16},{8,24},{16,0},{24,8},{1,17},{9,25},{17,1},{25,9},{2,18},{10... | collective-permute-start | bytes 2396168 | tf_op jit(solution)/shard_map/ppermute | solution.py:22
  49.2 1.6 %collective-permute-done.13.beside = bf16[2,1040,384]{2,1,0:T(8,128)(2,1)S(1)} collective-permute-done((bf16[2,1040,384]{2,1,0:T(8,128)(2,1)S(1)}, bf16[2,1040,384]{2,1,0:T(8,128)(2,1)S(1)}, u32[]{:S(2)}, u32[]{:S(2)}) %collective-permute-start.13) | collective-permute-done | bytes 1597472 | tf_op jit(solution)/shard_map/ppermute | solution.py:22
  50.9 0.2 fusion
  51.1 1.6 %collective-permute-start.14 = (bf16[1040,384]{1,0:T(8,128)(2,1)S(1)}, bf16[1040,384]{1,0:T(8,128)(2,1)S(1)}, u32[]{:S(2)}, u32[]{:S(2)}) collective-permute-start(bf16[1040,384]{1,0:T(8,128)(2,1)S(1)} %fusion), channel_id=1, source_target_pairs={{0,16},{8,24},{16,0},{24,8},{1,17},{9,25},{17,1},{25,9},{2,18},{10... | collective-permute-start | bytes 2396168 | tf_op jit(solution)/shard_map/ppermute | solution.py:22
  52.7 15.7 %collective-permute-done.5.across = bf16[1040,384]{1,0:T(8,128)(2,1)S(1)} collective-permute-done((bf16[1040,384]{1,0:T(8,128)(2,1)S(1)}, bf16[1040,384]{1,0:T(8,128)(2,1)S(1)}, u32[]{:S(2)}, u32[]{:S(2)}) %collective-permute-start.5) | collective-permute-done | bytes 798752 | tf_op jit(solution)/shard_map/ppermute | solution.py:22
  68.4 4.6 %copy-done = bf16[16,192,2048]{2,1,0:T(8,128)(2,1)S(1)} copy-done((bf16[16,192,2048]{2,1,0:T(8,128)(2,1)S(1)}, bf16[16,192,2048]{2,1,0:T(8,128)(2,1)}, u32[]{:S(2)}) %copy-start) | copy-done | bytes 12582936
  73.0 8.5 %down.2 = (bf16[512,512]{1,0:T(8,128)(2,1)S(1)}, bf16[512,512]{1,0:T(8,128)(2,1)S(1)}, bf16[2,512,512]{2,1,0:T(8,128)(2,1)S(1)}) custom-call(s32[2]{0:T(128)S(1)} %pad_add_fusion.2.place, s32[16]{0:T(128)S(1)} %get-tuple-element.21.meta, s32[32,128]{1,0:T(8,128)S(1)} %pad_add_fusion.ids, s32[16,512]{1,0:T(8,128)S(1)} %get-tuple-element.22.pos, ...), custom_call_target="tpu_custom_call" | custom-call | flops 2147483648 | bytes 12582912 | tf_op jit(solution)/shard_map/down/pallas_call | solution.py:172
  81.6 3.5 %collective-permute-done.14.across = bf16[1040,384]{1,0:T(8,128)(2,1)S(1)} collective-permute-done((bf16[1040,384]{1,0:T(8,128)(2,1)S(1)}, bf16[1040,384]{1,0:T(8,128)(2,1)S(1)}, u32[]{:S(2)}, u32[]{:S(2)}) %collective-permute-start.14) | collective-permute-done | bytes 798752 | tf_op jit(solution)/shard_map/ppermute | solution.py:22
  85.0 4.6 %copy-done.1 = bf16[16,192,2048]{2,1,0:T(8,128)(2,1)S(1)} copy-done((bf16[16,192,2048]{2,1,0:T(8,128)(2,1)S(1)}, bf16[16,192,2048]{2,1,0:T(8,128)(2,1)}, u32[]{:S(2)}) %copy-start.1) | copy-done | bytes 12582936
  89.6 8.7 %down.3 = (bf16[512,512]{1,0:T(8,128)(2,1)S(1)}, bf16[512,512]{1,0:T(8,128)(2,1)S(1)}, bf16[2,512,512]{2,1,0:T(8,128)(2,1)S(1)}) custom-call(s32[2]{0:T(128)S(1)} %pad_add_fusion.2.place, s32[16]{0:T(128)S(1)} %get-tuple-element.29.meta, s32[32,128]{1,0:T(8,128)S(1)} %collective-permute-done.11.ids, s32[16,512]{1,0:T(8,128)S(1)} %get-tuple-element.30.pos, ...), custom_call_target="tpu_custom_call" | custom-call | flops 2147483648 | bytes 12582912 | tf_op jit(solution)/shard_map/down/pallas_call | solution.py:172
  98.4 0.1 fusion.5
  98.6 1.6 %collective-permute-start.7 = (bf16[512,512]{1,0:T(8,128)(2,1)S(1)}, bf16[512,512]{1,0:T(8,128)(2,1)S(1)}, u32[]{:S(2)}, u32[]{:S(2)}) collective-permute-start(bf16[512,512]{1,0:T(8,128)(2,1)S(1)} %fusion.5), channel_id=1, source_target_pairs={{0,16},{8,24},{16,0},{24,8},{1,17},{9,25},{17,1},{25,9},{2,18},{10... | collective-permute-start | bytes 1572872 | tf_op jit(solution)/shard_map/ppermute | solution.py:22
  100.2 0.9 collective-permute-done.15
  101.1 0.1 fusion.2
  101.2 1.6 %collective-permute-start.16 = (bf16[512,512]{1,0:T(8,128)(2,1)S(1)}, bf16[512,512]{1,0:T(8,128)(2,1)S(1)}, u32[]{:S(2)}, u32[]{:S(2)}) collective-permute-start(bf16[512,512]{1,0:T(8,128)(2,1)S(1)} %fusion.2), channel_id=1, source_target_pairs={{0,16},{8,24},{16,0},{24,8},{1,17},{9,25},{17,1},{25,9},{2,18},{10... | collective-permute-start | bytes 1572872 | tf_op jit(solution)/shard_map/ppermute | solution.py:22
  102.8 10.6 %collective-permute-done.7 = bf16[512,512]{1,0:T(8,128)(2,1)S(1)} collective-permute-done((bf16[512,512]{1,0:T(8,128)(2,1)S(1)}, bf16[512,512]{1,0:T(8,128)(2,1)S(1)}, u32[]{:S(2)}, u32[]{:S(2)}) %collective-permute-start.7) | collective-permute-done | bytes 524320 | tf_op jit(solution)/shard_map/ppermute | solution.py:22
  113.4 0.2 fusion.7
  113.7 1.3 collective-permute-start.8
  115.0 1.4 %collective-permute-start.10 = (bf16[128,512]{1,0:T(8,128)(2,1)S(1)}, bf16[128,512]{1,0:T(8,128)(2,1)S(1)}, u32[]{:S(2)}, u32[]{:S(2)}) collective-permute-start(bf16[128,512]{1,0:T(8,128)(2,1)S(1)} %get-tuple-element.38), channel_id=1, source_target_pairs={{0,6},{1,7},{2,4},{3,5},{4,2},{5,3},{6,0},{7,1},{8,14},{9,15},{10,... | collective-permute-start | bytes 393224 | tf_op jit(solution)/shard_map/ppermute | solution.py:22
  116.4 0.8 collective-permute-start.9
  117.2 7.0 %collective-permute-done.16 = bf16[512,512]{1,0:T(8,128)(2,1)S(1)} collective-permute-done((bf16[512,512]{1,0:T(8,128)(2,1)S(1)}, bf16[512,512]{1,0:T(8,128)(2,1)S(1)}, u32[]{:S(2)}, u32[]{:S(2)}) %collective-permute-start.16) | collective-permute-done | bytes 524320 | tf_op jit(solution)/shard_map/ppermute | solution.py:22
  124.2 0.2 fusion.4
  124.4 0.6 collective-permute-start.17
  125.0 3.4 %collective-permute-start.20 = (bf16[128,512]{1,0:T(8,128)(2,1)S(1)}, bf16[128,512]{1,0:T(8,128)(2,1)S(1)}, u32[]{:S(2)}, u32[]{:S(2)}) collective-permute-start(bf16[128,512]{1,0:T(8,128)(2,1)S(1)} %get-tuple-element.41), channel_id=1, source_target_pairs={{0,7},{1,6},{2,5},{3,4},{4,3},{5,2},{6,1},{7,0},{8,15},{9,14},{10,... | collective-permute-start | bytes 393224 | tf_op jit(solution)/shard_map/ppermute | solution.py:22
  128.4 2.9 %collective-permute-start.18 = (bf16[128,512]{1,0:T(8,128)(2,1)S(1)}, bf16[128,512]{1,0:T(8,128)(2,1)S(1)}, u32[]{:S(2)}, u32[]{:S(2)}) collective-permute-start(bf16[128,512]{1,0:T(8,128)(2,1)S(1)} %get-tuple-element.43), channel_id=1, source_target_pairs={{0,5},{1,4},{2,7},{3,6},{4,1},{5,0},{6,3},{7,2},{8,13},{9,12},{10,... | collective-permute-start | bytes 393224 | tf_op jit(solution)/shard_map/ppermute | solution.py:22
  131.3 2.8 %collective-permute-done.20 = bf16[128,512]{1,0:T(8,128)(2,1)S(1)} collective-permute-done((bf16[128,512]{1,0:T(8,128)(2,1)S(1)}, bf16[128,512]{1,0:T(8,128)(2,1)S(1)}, u32[]{:S(2)}, u32[]{:S(2)}) %collective-permute-start.20) | collective-permute-done | bytes 131104 | tf_op jit(solution)/shard_map/ppermute | solution.py:22
  134.1 3.2 %collective-permute-done.19 = bf16[128,512]{1,0:T(8,128)(2,1)S(1)} collective-permute-done((bf16[128,512]{1,0:T(8,128)(2,1)S(1)}, bf16[128,512]{1,0:T(8,128)(2,1)S(1)}, u32[]{:S(2)}, u32[]{:S(2)}) %collective-permute-start.19) | collective-permute-done | bytes 131104 | tf_op jit(solution)/shard_map/ppermute | solution.py:22
  137.3 1.8 %collective-permute-done.18 = bf16[128,512]{1,0:T(8,128)(2,1)S(1)} collective-permute-done((bf16[128,512]{1,0:T(8,128)(2,1)S(1)}, bf16[128,512]{1,0:T(8,128)(2,1)S(1)}, u32[]{:S(2)}, u32[]{:S(2)}) %collective-permute-start.18) | collective-permute-done | bytes 131104 | tf_op jit(solution)/shard_map/ppermute | solution.py:22
  139.1 0.8 add_convert_fusion
  (20 shorter events, 0.3 us)
Async XLA Ops:
  0.0 22.7 %copy-start.2 = (bf16[512,128]{1,0:T(8,128)(2,1)S(1)}, bf16[512,128]{1,0:T(8,128)(2,1)}, u32[]{:S(2)}) copy-start(bf16[512,128]{1,0:T(8,128)(2,1)} %router.3) | copy-start | bytes 393220
  0.0 5.9 %collective-permute-start = (s32[8,128]{1,0:T(8,128)}, s32[8,128]{1,0:T(8,128)S(1)}, u32[]{:S(2)}, u32[]{:S(2)}) collective-permute-start(s32[8,128]{1,0:T(8,128)} %bitcast.33), channel_id=1, source_target_pairs={{0,4},{1,5},{2,6},{3,7},{4,0},{5,1},{6,2},{7,3},{8,12},{9,13},{10,... | collective-permute-start | bytes 12296 | tf_op jit(solution)/shard_map/ppermute | solution.py:22
  4.1 8.9 %collective-permute-start.2 = (bf16[128,512]{1,0:T(8,128)(2,1)}, bf16[128,512]{1,0:T(8,128)(2,1)S(1)}, u32[]{:S(2)}, u32[]{:S(2)}) collective-permute-start(bf16[128,512]{1,0:T(8,128)(2,1)} %param.5), channel_id=1, source_target_pairs={{0,4},{1,5},{2,6},{3,7},{4,0},{5,1},{6,2},{7,3},{8,12},{9,13},{10,... | collective-permute-start | bytes 393224 | tf_op jit(solution)/shard_map/ppermute | solution.py:22
  6.6 7.5 %collective-permute-start.1 = (s32[16,128]{1,0:T(8,128)S(1)}, s32[16,128]{1,0:T(8,128)S(1)}, u32[]{:S(2)}, u32[]{:S(2)}) collective-permute-start(s32[16,128]{1,0:T(8,128)S(1)} %pad_add_fusion.1), channel_id=1, source_target_pairs={{0,2},{1,3},{2,0},{3,1},{4,6},{5,7},{6,4},{7,5},{8,10},{9,11},{10,... | collective-permute-start | bytes 24584 | tf_op jit(solution)/shard_map/ppermute | solution.py:22
  13.9 7.3 %collective-permute-start.3 = (bf16[256,512]{1,0:T(8,128)(2,1)S(1)}, bf16[256,512]{1,0:T(8,128)(2,1)S(1)}, u32[]{:S(2)}, u32[]{:S(2)}) collective-permute-start(bf16[256,512]{1,0:T(8,128)(2,1)S(1)} %pad_maximum_fusion), channel_id=1, source_target_pairs={{0,2},{1,3},{2,0},{3,1},{4,6},{5,7},{6,4},{7,5},{8,10},{9,11},{10,... | collective-permute-start | bytes 786440 | tf_op jit(solution)/shard_map/ppermute | solution.py:22
  21.2 15.7 %collective-permute-start.12 = (bf16[512,512]{1,0:T(8,128)(2,1)S(1)}, bf16[512,512]{1,0:T(8,128)(2,1)S(1)}, u32[]{:S(2)}, u32[]{:S(2)}) collective-permute-start(bf16[512,512]{1,0:T(8,128)(2,1)S(1)} %constant_dynamic-update-slice_fusion.tokens), channel_id=1, source_target_pairs={{0,1},{1,0},{2,3},{3,2},{4,5},{5,4},{6,7},{7,6},{8,9},{9,8},{10,11... | collective-permute-start | bytes 1572872 | tf_op jit(solution)/shard_map/ppermute | solution.py:22
  33.0 14.4 %collective-permute-start.4 = (bf16[2,1040,384]{2,1,0:T(8,128)(2,1)S(1)}, bf16[2,1040,384]{2,1,0:T(8,128)(2,1)S(1)}, u32[]{:S(2)}, u32[]{:S(2)}) collective-permute-start(bf16[2,1040,384]{2,1,0:T(8,128)(2,1)S(1)} %get-tuple-element.24), channel_id=1, source_target_pairs={{0,8},{8,0},{16,24},{24,16},{1,9},{9,1},{17,25},{25,17},{2,10},{10... | collective-permute-start | bytes 4792328 | tf_op jit(solution)/shard_map/ppermute | solution.py:22
  33.1 3.8 %collective-permute-start.11 = (s32[32,128]{1,0:T(8,128)S(1)}, s32[32,128]{1,0:T(8,128)S(1)}, u32[]{:S(2)}, u32[]{:S(2)}) collective-permute-start(s32[32,128]{1,0:T(8,128)S(1)} %pad_add_fusion.ids), channel_id=1, source_target_pairs={{0,1},{1,0},{2,3},{3,2},{4,5},{5,4},{6,7},{7,6},{8,9},{9,8},{10,11... | collective-permute-start | bytes 49160 | tf_op jit(solution)/shard_map/ppermute | solution.py:22
  47.4 3.5 %collective-permute-start.13 = (bf16[2,1040,384]{2,1,0:T(8,128)(2,1)S(1)}, bf16[2,1040,384]{2,1,0:T(8,128)(2,1)S(1)}, u32[]{:S(2)}, u32[]{:S(2)}) collective-permute-start(bf16[2,1040,384]{2,1,0:T(8,128)(2,1)S(1)} %get-tuple-element.32), channel_id=1, source_target_pairs={{0,8},{8,0},{16,24},{24,16},{1,9},{9,1},{17,25},{25,17},{2,10},{10... | collective-permute-start | bytes 4792328 | tf_op jit(solution)/shard_map/ppermute | solution.py:22
  47.7 20.7 %collective-permute-start.5 = (bf16[1040,384]{1,0:T(8,128)(2,1)S(1)}, bf16[1040,384]{1,0:T(8,128)(2,1)S(1)}, u32[]{:S(2)}, u32[]{:S(2)}) collective-permute-start(bf16[1040,384]{1,0:T(8,128)(2,1)S(1)} %fusion.1), channel_id=1, source_target_pairs={{0,16},{8,24},{16,0},{24,8},{1,17},{9,25},{17,1},{25,9},{2,18},{10... | collective-permute-start | bytes 2396168 | tf_op jit(solution)/shard_map/ppermute | solution.py:22
  51.1 34.0 %collective-permute-start.14 = (bf16[1040,384]{1,0:T(8,128)(2,1)S(1)}, bf16[1040,384]{1,0:T(8,128)(2,1)S(1)}, u32[]{:S(2)}, u32[]{:S(2)}) collective-permute-start(bf16[1040,384]{1,0:T(8,128)(2,1)S(1)} %fusion), channel_id=1, source_target_pairs={{0,16},{8,24},{16,0},{24,8},{1,17},{9,25},{17,1},{25,9},{2,18},{10... | collective-permute-start | bytes 2396168 | tf_op jit(solution)/shard_map/ppermute | solution.py:22
  68.4 4.6 %copy-start = (bf16[16,192,2048]{2,1,0:T(8,128)(2,1)S(1)}, bf16[16,192,2048]{2,1,0:T(8,128)(2,1)}, u32[]{:S(2)}) copy-start(bf16[16,192,2048]{2,1,0:T(8,128)(2,1)} %weight.7) | copy-start | bytes 37748740
  81.5 16.9 %collective-permute-start.6 = (bf16[2,512,512]{2,1,0:T(8,128)(2,1)S(1)}, bf16[2,512,512]{2,1,0:T(8,128)(2,1)S(1)}, u32[]{:S(2)}, u32[]{:S(2)}) collective-permute-start(bf16[2,512,512]{2,1,0:T(8,128)(2,1)S(1)} %get-tuple-element.27), channel_id=1, source_target_pairs={{0,8},{8,0},{16,24},{24,16},{1,9},{9,1},{17,25},{25,17},{2,10},{10... | collective-permute-start | bytes 3145736 | tf_op jit(solution)/shard_map/ppermute | solution.py:22
  85.0 4.6 %copy-start.1 = (bf16[16,192,2048]{2,1,0:T(8,128)(2,1)S(1)}, bf16[16,192,2048]{2,1,0:T(8,128)(2,1)}, u32[]{:S(2)}) copy-start(bf16[16,192,2048]{2,1,0:T(8,128)(2,1)} %weight.7) | copy-start | bytes 37748740
  98.3 2.7 %collective-permute-start.15 = (bf16[2,512,512]{2,1,0:T(8,128)(2,1)S(1)}, bf16[2,512,512]{2,1,0:T(8,128)(2,1)S(1)}, u32[]{:S(2)}, u32[]{:S(2)}) collective-permute-start(bf16[2,512,512]{2,1,0:T(8,128)(2,1)S(1)} %get-tuple-element.35), channel_id=1, source_target_pairs={{0,8},{8,0},{16,24},{24,16},{1,9},{9,1},{17,25},{25,17},{2,10},{10... | collective-permute-start | bytes 3145736 | tf_op jit(solution)/shard_map/ppermute | solution.py:22
  98.6 14.9 %collective-permute-start.7 = (bf16[512,512]{1,0:T(8,128)(2,1)S(1)}, bf16[512,512]{1,0:T(8,128)(2,1)S(1)}, u32[]{:S(2)}, u32[]{:S(2)}) collective-permute-start(bf16[512,512]{1,0:T(8,128)(2,1)S(1)} %fusion.5), channel_id=1, source_target_pairs={{0,16},{8,24},{16,0},{24,8},{1,17},{9,25},{17,1},{25,9},{2,18},{10... | collective-permute-start | bytes 1572872 | tf_op jit(solution)/shard_map/ppermute | solution.py:22
  101.2 23.0 %collective-permute-start.16 = (bf16[512,512]{1,0:T(8,128)(2,1)S(1)}, bf16[512,512]{1,0:T(8,128)(2,1)S(1)}, u32[]{:S(2)}, u32[]{:S(2)}) collective-permute-start(bf16[512,512]{1,0:T(8,128)(2,1)S(1)} %fusion.2), channel_id=1, source_target_pairs={{0,16},{8,24},{16,0},{24,8},{1,17},{9,25},{17,1},{25,9},{2,18},{10... | collective-permute-start | bytes 1572872 | tf_op jit(solution)/shard_map/ppermute | solution.py:22
  113.7 14.7 %collective-permute-start.8 = (bf16[128,512]{1,0:T(8,128)(2,1)S(1)}, bf16[128,512]{1,0:T(8,128)(2,1)S(1)}, u32[]{:S(2)}, u32[]{:S(2)}) collective-permute-start(bf16[128,512]{1,0:T(8,128)(2,1)S(1)} %get-tuple-element.37), channel_id=1, source_target_pairs={{0,4},{1,5},{2,6},{3,7},{4,0},{5,1},{6,2},{7,3},{8,12},{9,13},{10,... | collective-permute-start | bytes 393224 | tf_op jit(solution)/shard_map/ppermute | solution.py:22
  115.0 13.4 %collective-permute-start.10 = (bf16[128,512]{1,0:T(8,128)(2,1)S(1)}, bf16[128,512]{1,0:T(8,128)(2,1)S(1)}, u32[]{:S(2)}, u32[]{:S(2)}) collective-permute-start(bf16[128,512]{1,0:T(8,128)(2,1)S(1)} %get-tuple-element.38), channel_id=1, source_target_pairs={{0,6},{1,7},{2,4},{3,5},{4,2},{5,3},{6,0},{7,1},{8,14},{9,15},{10,... | collective-permute-start | bytes 393224 | tf_op jit(solution)/shard_map/ppermute | solution.py:22
  116.4 14.9 %collective-permute-start.9 = (bf16[128,512]{1,0:T(8,128)(2,1)S(1)}, bf16[128,512]{1,0:T(8,128)(2,1)S(1)}, u32[]{:S(2)}, u32[]{:S(2)}) collective-permute-start(bf16[128,512]{1,0:T(8,128)(2,1)S(1)} %get-tuple-element.39), channel_id=1, source_target_pairs={{0,2},{1,3},{2,0},{3,1},{4,6},{5,7},{6,4},{7,5},{8,10},{9,11},{10,... | collective-permute-start | bytes 393224 | tf_op jit(solution)/shard_map/ppermute | solution.py:22
  124.4 6.8 %collective-permute-start.17 = (bf16[128,512]{1,0:T(8,128)(2,1)S(1)}, bf16[128,512]{1,0:T(8,128)(2,1)S(1)}, u32[]{:S(2)}, u32[]{:S(2)}) collective-permute-start(bf16[128,512]{1,0:T(8,128)(2,1)S(1)} %get-tuple-element.40), channel_id=1, source_target_pairs={{0,1},{1,0},{2,3},{3,2},{4,5},{5,4},{6,7},{7,6},{8,9},{9,8},{10,11... | collective-permute-start | bytes 393224 | tf_op jit(solution)/shard_map/ppermute | solution.py:22
  125.0 9.1 %collective-permute-start.20 = (bf16[128,512]{1,0:T(8,128)(2,1)S(1)}, bf16[128,512]{1,0:T(8,128)(2,1)S(1)}, u32[]{:S(2)}, u32[]{:S(2)}) collective-permute-start(bf16[128,512]{1,0:T(8,128)(2,1)S(1)} %get-tuple-element.41), channel_id=1, source_target_pairs={{0,7},{1,6},{2,5},{3,4},{4,3},{5,2},{6,1},{7,0},{8,15},{9,14},{10,... | collective-permute-start | bytes 393224 | tf_op jit(solution)/shard_map/ppermute | solution.py:22
  128.4 8.9 %collective-permute-start.19 = (bf16[128,512]{1,0:T(8,128)(2,1)S(1)}, bf16[128,512]{1,0:T(8,128)(2,1)S(1)}, u32[]{:S(2)}, u32[]{:S(2)}) collective-permute-start(bf16[128,512]{1,0:T(8,128)(2,1)S(1)} %get-tuple-element.42), channel_id=1, source_target_pairs={{0,3},{1,2},{2,1},{3,0},{4,7},{5,6},{6,5},{7,4},{8,11},{9,10},{10,... | collective-permute-start | bytes 393224 | tf_op jit(solution)/shard_map/ppermute | solution.py:22
  128.4 10.7 %collective-permute-start.18 = (bf16[128,512]{1,0:T(8,128)(2,1)S(1)}, bf16[128,512]{1,0:T(8,128)(2,1)S(1)}, u32[]{:S(2)}, u32[]{:S(2)}) collective-permute-start(bf16[128,512]{1,0:T(8,128)(2,1)S(1)} %get-tuple-element.43), channel_id=1, source_target_pairs={{0,5},{1,4},{2,7},{3,6},{4,1},{5,0},{6,3},{7,2},{8,13},{9,12},{10,... | collective-permute-start | bytes 393224 | tf_op jit(solution)/shard_map/ppermute | solution.py:22

commit v2 on v1

--- a/solution.py
+++ b/solution.py
@@ -11,6 +11,9 @@
 TOPK = 8
 CAP = 16
 GROUP = 4
+PARTS = 2
+GATE_VMEM = 40
+DOWN_VMEM = 54
 TILE = GROUP * CAP
 ALIGN = 16
 F32 = jnp.float32
@@ -22,8 +25,8 @@
     return lax.ppermute(x, axis, [(i, i ^ mask) for i in range(size)])
 
 
-def gate_up_kernel(place, ids, tokens, router, weight, near, far, send, pos, meta, buffer, arrived, *,
-                   blocks, local_experts):
+def gate_up_kernel(place, *refs, blocks, local_experts):
+    block, (router, weight, near, far, send, pos, ids, meta, tokens, buffer, arrived) = refs[:blocks], refs[blocks:]
     total = tokens.shape[0]
     tok = total // blocks
     copies = [pltpu.make_async_copy(weight.at[e], buffer.at[e], arrived.at[e]) for e in range(local_experts)]
@@ -38,6 +41,8 @@
     ranks, hots, chosen = [], [], []
     for b in range(blocks):
         hot = jnp.zeros(expert.shape, F32)
+        tokens[b * tok:(b + 1) * tok, :] = block[b][:tok, :]
+        ids[b * TOPK:(b + 1) * TOPK, :] = block[b][tok:, :tok].astype(F32).astype(jnp.int32)
         logits = jnp.dot(tokens[b * tok:(b + 1) * tok, :], router[...], preferred_element_type=F32).T
         for k in range(TOPK):
             row = ids[b * TOPK + k:b * TOPK + k + 1, :]
@@ -90,25 +95,28 @@
 HBM = pl.BlockSpec(memory_space=pltpu.HBM)
 
 
-def gate_up(place, ids, tokens, router, weight, blocks):
-    total, width = tokens.shape
+def gate_up(place, block, router, weight, tok):
+    blocks = len(block)
+    total, width = blocks * tok, block[0].shape[1]
     local_experts, _, _, units = weight.shape
     half = units // 2
     rows = local_experts * TILE + 2 * TOPK
     return pl.pallas_call(
         functools.partial(gate_up_kernel, blocks=blocks, local_experts=local_experts),
-        in_specs=[SMEM, VMEM, VMEM, VMEM, HBM],
-        out_specs=[VMEM, VMEM, VMEM, VMEM, SMEM],
-        scratch_shapes=[pltpu.VMEM(weight.shape, BF16), pltpu.SemaphoreType.DMA((local_experts,))],
+        in_specs=[SMEM] + [VMEM] * (blocks + 1) + [HBM],
+        out_specs=[VMEM, VMEM, VMEM, VMEM, VMEM, SMEM],
+        scratch_shapes=[pltpu.VMEM((total, width), BF16), pltpu.VMEM(weight.shape, BF16),
+                        pltpu.SemaphoreType.DMA((local_experts,))],
         out_shape=[jax.ShapeDtypeStruct((rows, half), BF16), jax.ShapeDtypeStruct((rows, half), BF16),
                    jax.ShapeDtypeStruct((2, rows, half), BF16),
                    jax.ShapeDtypeStruct((max(local_experts, 8), total), jnp.int32),
+                   jax.ShapeDtypeStruct((blocks * TOPK, tok), jnp.int32),
                    jax.ShapeDtypeStruct((max(local_experts, 8),), jnp.int32)],
-        compiler_params=pltpu.CompilerParams(vmem_limit_bytes=36 * 1024 * 1024),
+        compiler_params=pltpu.CompilerParams(vmem_limit_bytes=GATE_VMEM * 1024 * 1024),
         cost_estimate=pl.CostEstimate(flops=6 * rows * width * units, bytes_accessed=2 * weight.size,
                                       transcendentals=0),
         name="gate_up",
-    )(place, ids, tokens, router, weight)
+    )(place, *block, router, weight)
 
 
 def down_kernel(place, meta, ids, pos, near, beside, across, weight, keep, far, send,
@@ -178,7 +186,7 @@
                         pltpu.SemaphoreType.DMA((local_experts,))],
         out_shape=[jax.ShapeDtypeStruct((total, width), BF16), jax.ShapeDtypeStruct((total, width), BF16),
                    jax.ShapeDtypeStruct((2, total, width), BF16)],
-        compiler_params=pltpu.CompilerParams(vmem_limit_bytes=36 * 1024 * 1024),
+        compiler_params=pltpu.CompilerParams(vmem_limit_bytes=DOWN_VMEM * 1024 * 1024),
         cost_estimate=pl.CostEstimate(flops=8 * total * cap * width, bytes_accessed=2 * weight.size,
                                       transcendentals=0),
         name="down",
@@ -193,17 +201,13 @@
 
 
 def gather_wide(x, size):
-    chunks, order = [x], [[0]]
+    pieces = {0: x}
     bit = size // 2
     while bit:
-        moved = [swap(p, "wide", bit) for p in chunks]
-        flipped = [[j | bit for j in o] for o in order]
-        if len(order[0]) < GROUP:
-            chunks, order = [jnp.concatenate([chunks[0], moved[0]], axis=0)], [order[0] + flipped[0]]
-        else:
-            chunks, order = chunks + moved, order + flipped
+        for j, p in list(pieces.items()):
+            pieces[j | bit] = swap(p, "wide", bit)
         bit //= 2
-    return chunks, order
+    return pieces
 
 
 def local(normed, router_weight, gate_up_weight, down_weight, expert_ids):
@@ -212,27 +216,34 @@
     size = lax.axis_size("wide")
     mine = lax.axis_index("narrow")
     place = jnp.stack([mine, lax.axis_index("wide") * local_experts]).astype(jnp.int32)
-    ids, _ = gather_wide(expert_ids.T, size)
-    tokens, order = gather_wide(normed, size)
+    ids = jnp.pad(expert_ids.T.astype(BF16), ((0, 0), (0, width - tok)))
+    pieces = gather_wide(jnp.concatenate([normed, ids], axis=0), size)
+    groups = size // GROUP
+    order = [[c + groups * i for i in range(GROUP)] for c in range(groups)]
 
     stage = []
-    for c in range(len(order)):
-        near, far, send, pos, meta = gate_up(place, ids[c], tokens[c], router_weight, gate_up_weight, GROUP)
+    for c in range(groups):
+        near, far, send, pos, ids, meta = gate_up(
+            place, [pieces[j] for j in order[c]], router_weight, gate_up_weight, tok)
         beside = swap(send, "narrow", 1)
         far = add(far, beside[1])
         across = swap(far, "narrow", 2)
-        stage.append((near, beside, across, pos, meta))
+        stage.append((near, beside, across, pos, ids, meta))
     terms = []
-    for c in range(len(order)):
-        near, beside, across, pos, meta = stage[c]
-        keep, far, send = down(place, meta, ids[c], pos, near, beside, across, down_weight, GROUP, tok, width)
+    for c in range(groups):
+        near, beside, across, pos, ids, meta = stage[c]
+        keep, far, send = down(place, meta, ids, pos, near, beside, across, down_weight, GROUP, tok, width)
         beside = swap(send, "narrow", 1)
-        far = add(far, beside[1])
-        across = swap(far, "narrow", 2)
-        whole = add(keep, beside[0], across)
-        for i, j in enumerate(order[c]):
-            piece = whole[i * tok:(i + 1) * tok]
-            terms.append(swap(piece, "wide", j) if j else piece)
+        parts = PARTS if c == groups - 1 else 1
+        rows = GROUP * tok // parts
+        for p in range(parts):
+            own = slice(p * rows, (p + 1) * rows)
+            across = swap(add(far[own], beside[1, own]), "narrow", 2)
+            whole = add(keep[own], beside[0, own], across)
+            for i in range(GROUP // parts):
+                j = order[c][p * GROUP // parts + i]
+                piece = whole[i * tok:(i + 1) * tok]
+                terms.append(swap(piece, "wide", j) if j else piece)
     return add(*terms)
 
 

time: 140 us -> 146 us (1.043)
  starting transfers between devices: 25.2 us -> 31.3 us
  local copies, waits for them, and re-layouts: 10.2 us -> 5.44 us
  Pallas kernels: 38 us -> 42.4 us
    ppermute x21 -> x23, starting transfers between devices: 25.2 us -> 31.3 us  [swap(): return lax.ppermute(x, axis, [(i, i ^ mask) for i in range(size)])]
    unnamed x8 -> x38, local copies, waits for them, and re-layouts: 10.1 us -> 5.37 us
    pallas_call x2, Pallas kernels: 17.2 us -> 21.3 us  [down(): pl.pallas_call(functools.partial(down_kernel, blocks=blocks, local_expert...]
    ppermute x21 -> x23, waiting for transfers between devices: 62 us -> 62.9 us  [swap(): return lax.ppermute(x, axis, [(i, i ^ mask) for i in range(size)])]
  transfers between devices with their start and end apart: 21 -> 23, of which waited for: 13 -> 16; matrix products, arithmetic and copies ran while one was open for 3% -> 1% of each run, Pallas kernels for 27% -> 22%
where the time goes in v2:
time: 146 us
  waiting for transfers between devices  62.9 us (43%)
  Pallas kernels  42.4 us (29%)
  starting transfers between devices  31.3 us (21%)
  local copies, waits for them, and re-layouts  5.44 us (4%)
  other arithmetic  3.58 us (2%)
    ppermute x23, waiting for transfers between devices, swap(): return lax.ppermute(x, axis, [(i, i ^ mask) for i in range(size)])  62.9 us
    ppermute x23, starting transfers between devices, swap(): return lax.ppermute(x, axis, [(i, i ^ mask) for i in range(size)])  31.3 us
    pallas_call x2, Pallas kernels, down(): pl.pallas_call(functools.partial(down_kernel, blocks=blocks, local_expert...  21.3 us
    pallas_call x2, Pallas kernels, gate_up(): pl.pallas_call(functools.partial(gate_up_kernel, blocks=blocks, local_exp...  21.1 us
    unnamed x38, local copies, waits for them, and re-layouts  5.37 us
  transfers between devices with their start and end apart: 23, of which 16 were waited for; matrix products, arithmetic and copies ran while one was open for 1% of the time, Pallas kernels for 22%

profile of v2, /device:TPU:0, one launch (start us, length us, event | category | flops | bytes accessed | tf_op | source)
XLA Modules:
  0.0 145.8 jit_solution(17073789129406066967)
XLA Ops:
  0.0 0.7 convert_bitcast_fusion
  0.7 0.9 fusion.12.refs_0_
  1.6 4.1 %collective-permute-start.1 = (bf16[136,512]{1,0:T(8,128)(2,1)S(1)}, bf16[136,512]{1,0:T(8,128)(2,1)S(1)}, u32[]{:S(2)}, u32[]{:S(2)}) collective-permute-start(bf16[136,512]{1,0:T(8,128)(2,1)S(1)} %fusion.12.refs_0_), channel_id=1, source_target_pairs={{0,4},{1,5},{2,6},{3,7},{4,0},{5,1},{6,2},{7,3},{8,12},{9,13},{10,... | collective-permute-start | bytes 417800 | tf_op jit(solution)/shard_map/ppermute | solution.py:25
  5.7 1.6 %collective-permute-start = (bf16[136,512]{1,0:T(8,128)(2,1)S(1)}, bf16[136,512]{1,0:T(8,128)(2,1)S(1)}, u32[]{:S(2)}, u32[]{:S(2)}) collective-permute-start(bf16[136,512]{1,0:T(8,128)(2,1)S(1)} %fusion.12.refs_0_), channel_id=1, source_target_pairs={{0,2},{1,3},{2,0},{3,1},{4,6},{5,7},{6,4},{7,5},{8,10},{9,11},{10,... | collective-permute-start | bytes 417800 | tf_op jit(solution)/shard_map/ppermute | solution.py:25
  7.3 5.2 %collective-permute-done.1.refs_2_ = bf16[136,512]{1,0:T(8,128)(2,1)S(1)} collective-permute-done((bf16[136,512]{1,0:T(8,128)(2,1)S(1)}, bf16[136,512]{1,0:T(8,128)(2,1)S(1)}, u32[]{:S(2)}, u32[]{:S(2)}) %collective-permute-start.1) | collective-permute-done | bytes 139296 | tf_op jit(solution)/shard_map/ppermute | solution.py:25
  12.5 0.6 collective-permute-start.2
  13.1 1.5 %collective-permute-start.10 = (bf16[136,512]{1,0:T(8,128)(2,1)S(1)}, bf16[136,512]{1,0:T(8,128)(2,1)S(1)}, u32[]{:S(2)}, u32[]{:S(2)}) collective-permute-start(bf16[136,512]{1,0:T(8,128)(2,1)S(1)} %fusion.12.refs_0_), channel_id=1, source_target_pairs={{0,1},{1,0},{2,3},{3,2},{4,5},{5,4},{6,7},{7,6},{8,9},{9,8},{10,11... | collective-permute-start | bytes 417800 | tf_op jit(solution)/shard_map/ppermute | solution.py:25
  14.6 0.5 collective-permute-start.12
  15.1 1.5 %collective-permute-start.11 = (bf16[136,512]{1,0:T(8,128)(2,1)S(1)}, bf16[136,512]{1,0:T(8,128)(2,1)S(1)}, u32[]{:S(2)}, u32[]{:S(2)}) collective-permute-start(bf16[136,512]{1,0:T(8,128)(2,1)S(1)} %collective-permute-done.refs_1_), channel_id=1, source_target_pairs={{0,1},{1,0},{2,3},{3,2},{4,5},{5,4},{6,7},{7,6},{8,9},{9,8},{10,11... | collective-permute-start | bytes 417800 | tf_op jit(solution)/shard_map/ppermute | solution.py:25
  16.6 0.9 collective-permute-done.2.refs_3_
  17.6 1.5 %collective-permute-start.13 = (bf16[136,512]{1,0:T(8,128)(2,1)S(1)}, bf16[136,512]{1,0:T(8,128)(2,1)S(1)}, u32[]{:S(2)}, u32[]{:S(2)}) collective-permute-start(bf16[136,512]{1,0:T(8,128)(2,1)S(1)} %collective-permute-done.2.refs_3_), channel_id=1, source_target_pairs={{0,1},{1,0},{2,3},{3,2},{4,5},{5,4},{6,7},{7,6},{8,9},{9,8},{10,11... | collective-permute-start | bytes 417800 | tf_op jit(solution)/shard_map/ppermute | solution.py:25
  19.2 0.5 collective-permute-done.10.refs_0_
  19.7 3.0 %collective-permute-done.12.refs_2_ = bf16[136,512]{1,0:T(8,128)(2,1)S(1)} collective-permute-done((bf16[136,512]{1,0:T(8,128)(2,1)S(1)}, bf16[136,512]{1,0:T(8,128)(2,1)S(1)}, u32[]{:S(2)}, u32[]{:S(2)}) %collective-permute-start.12) | collective-permute-done | bytes 139296 | tf_op jit(solution)/shard_map/ppermute | solution.py:25
  22.6 3.0 %collective-permute-done.11.refs_1_ = bf16[136,512]{1,0:T(8,128)(2,1)S(1)} collective-permute-done((bf16[136,512]{1,0:T(8,128)(2,1)S(1)}, bf16[136,512]{1,0:T(8,128)(2,1)S(1)}, u32[]{:S(2)}, u32[]{:S(2)}) %collective-permute-start.11) | collective-permute-done | bytes 139296 | tf_op jit(solution)/shard_map/ppermute | solution.py:25
  25.6 1.8 %collective-permute-done.13.refs_3_ = bf16[136,512]{1,0:T(8,128)(2,1)S(1)} collective-permute-done((bf16[136,512]{1,0:T(8,128)(2,1)S(1)}, bf16[136,512]{1,0:T(8,128)(2,1)S(1)}, u32[]{:S(2)}, u32[]{:S(2)}) %collective-permute-start.13) | collective-permute-done | bytes 139296 | tf_op jit(solution)/shard_map/ppermute | solution.py:25
  27.4 0.9 copy-done.2
  28.3 10.5 %gate_up.3 = (bf16[1040,384]{1,0:T(8,128)(2,1)S(1)}, bf16[1040,384]{1,0:T(8,128)(2,1)S(1)}, bf16[2,1040,384]{2,1,0:T(8,128)(2,1)S(1)}, s32[16,512]{1,0:T(8,128)S...) custom-call(s32[2]{0:T(128)S(1)} %pad_add_fusion.place, bf16[136,512]{1,0:T(8,128)(2,1)S(1)} %collective-permute-done.10.refs_0_, ...), custom_call_target="tpu_custom_call" | custom-call | flops 2453667840 | bytes 25165824 | tf_op jit(solution)/shard_map/gate_up/pallas_call | solution.py:104
  38.8 0.9 copy-done.1
  39.7 0.6 copy-done.5
  40.3 0.6 copy-done.7
  40.9 0.5 copy-done.10
  41.4 10.6 %gate_up.2 = (bf16[1040,384]{1,0:T(8,128)(2,1)S(1)}, bf16[1040,384]{1,0:T(8,128)(2,1)S(1)}, bf16[2,1040,384]{2,1,0:T(8,128)(2,1)S(1)}, s32[16,512]{1,0:T(8,128)S...) custom-call(s32[2]{0:T(128)S(1)} %pad_add_fusion.place, bf16[136,512]{1,0:T(8,128)(2,1)S(1)} %fusion.12.refs_0_, ...), custom_call_target="tpu_custom_call" | custom-call | flops 2453667840 | bytes 25165824 | tf_op jit(solution)/shard_map/gate_up/pallas_call | solution.py:104
  52.1 0.6 collective-permute-start.3
  52.9 1.6 %collective-permute-start.15 = (bf16[1040,384]{1,0:T(8,128)(2,1)S(1)}, bf16[1040,384]{1,0:T(8,128)(2,1)S(1)}, u32[]{:S(2)}, u32[]{:S(2)}) collective-permute-start(bf16[1040,384]{1,0:T(8,128)(2,1)S(1)} %fusion), channel_id=1, source_target_pairs={{0,16},{8,24},{16,0},{24,8},{1,17},{9,25},{17,1},{25,9},{2,18},{10... | collective-permute-start | bytes 2396168 | tf_op jit(solution)/shard_map/ppermute | solution.py:25
  54.5 1.3 collective-permute-done.3.beside
  56.0 1.6 %collective-permute-start.4 = (bf16[1040,384]{1,0:T(8,128)(2,1)S(1)}, bf16[1040,384]{1,0:T(8,128)(2,1)S(1)}, u32[]{:S(2)}, u32[]{:S(2)}) collective-permute-start(bf16[1040,384]{1,0:T(8,128)(2,1)S(1)} %fusion.1), channel_id=1, source_target_pairs={{0,16},{8,24},{16,0},{24,8},{1,17},{9,25},{17,1},{25,9},{2,18},{10... | collective-permute-start | bytes 2396168 | tf_op jit(solution)/shard_map/ppermute | solution.py:25
  57.6 16.0 %collective-permute-done.15.across = bf16[1040,384]{1,0:T(8,128)(2,1)S(1)} collective-permute-done((bf16[1040,384]{1,0:T(8,128)(2,1)S(1)}, bf16[1040,384]{1,0:T(8,128)(2,1)S(1)}, u32[]{:S(2)}, u32[]{:S(2)}) %collective-permute-start.15) | collective-permute-done | bytes 798752 | tf_op jit(solution)/shard_map/ppermute | solution.py:25
  73.6 0.9 copy-done.14
  74.5 10.6 %down.3 = (bf16[512,512]{1,0:T(8,128)(2,1)}, bf16[512,512]{1,0:T(8,128)(2,1)}, bf16[2,512,512]{2,1,0:T(8,128)(2,1)}) custom-call(s32[2]{0:T(128)} %copy-done.8, s32[16]{0:T(128)} %copy-done.10, s32[32,128]{1,0:T(8,128)} %copy-done.7, s32[16,512]{1,0:T(8,128)} %copy-done.5, bf16[1040,384]{1,0:T(8,128)(2,1)} %copy-done.1, bf16[2,1040,384]{2,1,0:T(8,128)(2,1)} %copy-done.12, ...), custom_call_target="tpu_custom_call" | custom-call | flops 2147483648 | bytes 12582912 | tf_op jit(solution)/shard_map/down/pallas_call | solution.py:180
  85.2 4.6 %collective-permute-done.4.across = bf16[1040,384]{1,0:T(8,128)(2,1)S(1)} collective-permute-done((bf16[1040,384]{1,0:T(8,128)(2,1)S(1)}, bf16[1040,384]{1,0:T(8,128)(2,1)S(1)}, u32[]{:S(2)}, u32[]{:S(2)}) %collective-permute-start.4) | collective-permute-done | bytes 798752 | tf_op jit(solution)/shard_map/ppermute | solution.py:25
  89.8 0.9 copy-done.13
  90.7 10.7 %down.2 = (bf16[512,512]{1,0:T(8,128)(2,1)}, bf16[512,512]{1,0:T(8,128)(2,1)}, bf16[2,512,512]{2,1,0:T(8,128)(2,1)}) custom-call(s32[2]{0:T(128)} %copy-done.8, s32[16]{0:T(128)} %copy-done.9, s32[32,128]{1,0:T(8,128)} %copy-done.6, s32[16,512]{1,0:T(8,128)} %copy-done.4, bf16[1040,384]{1,0:T(8,128)(2,1)} %copy-done, bf16[2,1040,384]{2,1,0:T(8,128)(2,1)} %copy-done.11, ...), custom_call_target="tpu_custom_call" | custom-call | flops 2147483648 | bytes 12582912 | tf_op jit(solution)/shard_map/down/pallas_call | solution.py:180
  101.7 1.6 %collective-permute-start.17 = (bf16[256,512]{1,0:T(8,128)(2,1)S(1)}, bf16[256,512]{1,0:T(8,128)(2,1)S(1)}, u32[]{:S(2)}, u32[]{:S(2)}) collective-permute-start(bf16[256,512]{1,0:T(8,128)(2,1)S(1)} %get-tuple-element.43), channel_id=1, source_target_pairs={{0,16},{8,24},{16,0},{24,8},{1,17},{9,25},{17,1},{25,9},{2,18},{10... | collective-permute-start | bytes 786440 | tf_op jit(solution)/shard_map/ppermute | solution.py:25
  103.2 0.5 collective-permute-start.20
  103.7 0.6 collective-permute-done.5
  104.5 1.6 %collective-permute-start.6 = (bf16[512,512]{1,0:T(8,128)(2,1)S(1)}, bf16[512,512]{1,0:T(8,128)(2,1)S(1)}, u32[]{:S(2)}, u32[]{:S(2)}) collective-permute-start(bf16[512,512]{1,0:T(8,128)(2,1)S(1)} %fusion.2), channel_id=1, source_target_pairs={{0,16},{8,24},{16,0},{24,8},{1,17},{9,25},{17,1},{25,9},{2,18},{10... | collective-permute-start | bytes 1572872 | tf_op jit(solution)/shard_map/ppermute | solution.py:25
  106.1 4.8 %collective-permute-done.17 = bf16[256,512]{1,0:T(8,128)(2,1)S(1)} collective-permute-done((bf16[256,512]{1,0:T(8,128)(2,1)S(1)}, bf16[256,512]{1,0:T(8,128)(2,1)S(1)}, u32[]{:S(2)}, u32[]{:S(2)}) %collective-permute-start.17) | collective-permute-done | bytes 262176 | tf_op jit(solution)/shard_map/ppermute | solution.py:25
  110.9 5.6 %collective-permute-done.20 = bf16[256,512]{1,0:T(8,128)(2,1)S(1)} collective-permute-done((bf16[256,512]{1,0:T(8,128)(2,1)S(1)}, bf16[256,512]{1,0:T(8,128)(2,1)S(1)}, u32[]{:S(2)}, u32[]{:S(2)}) %collective-permute-start.20) | collective-permute-done | bytes 262176 | tf_op jit(solution)/shard_map/ppermute | solution.py:25
  116.8 1.6 %collective-permute-start.18 = (bf16[128,512]{1,0:T(8,128)(2,1)S(1)}, bf16[128,512]{1,0:T(8,128)(2,1)S(1)}, u32[]{:S(2)}, u32[]{:S(2)}) collective-permute-start(bf16[128,512]{1,0:T(8,128)(2,1)S(1)} %get-tuple-element.48), channel_id=1, source_target_pairs={{0,1},{1,0},{2,3},{3,2},{4,5},{5,4},{6,7},{7,6},{8,9},{9,8},{10,11... | collective-permute-start | bytes 393224 | tf_op jit(solution)/shard_map/ppermute | solution.py:25
  118.8 4.2 %collective-permute-start.21 = (bf16[128,512]{1,0:T(8,128)(2,1)S(1)}, bf16[128,512]{1,0:T(8,128)(2,1)S(1)}, u32[]{:S(2)}, u32[]{:S(2)}) collective-permute-start(bf16[128,512]{1,0:T(8,128)(2,1)S(1)} %get-tuple-element.50), channel_id=1, source_target_pairs={{0,5},{1,4},{2,7},{3,6},{4,1},{5,0},{6,3},{7,2},{8,13},{9,12},{10,... | collective-permute-start | bytes 393224 | tf_op jit(solution)/shard_map/ppermute | solution.py:25
  122.9 1.3 collective-permute-start.22
  124.2 3.1 %collective-permute-done.6 = bf16[512,512]{1,0:T(8,128)(2,1)S(1)} collective-permute-done((bf16[512,512]{1,0:T(8,128)(2,1)S(1)}, bf16[512,512]{1,0:T(8,128)(2,1)S(1)}, u32[]{:S(2)}, u32[]{:S(2)}) %collective-permute-start.6) | collective-permute-done | bytes 524320 | tf_op jit(solution)/shard_map/ppermute | solution.py:25
  127.5 0.5 collective-permute-start.7
  128.0 4.4 %collective-permute-start.9 = (bf16[128,512]{1,0:T(8,128)(2,1)S(1)}, bf16[128,512]{1,0:T(8,128)(2,1)S(1)}, u32[]{:S(2)}, u32[]{:S(2)}) collective-permute-start(bf16[128,512]{1,0:T(8,128)(2,1)S(1)} %get-tuple-element.46), channel_id=1, source_target_pairs={{0,6},{1,7},{2,4},{3,5},{4,2},{5,3},{6,0},{7,1},{8,14},{9,15},{10,... | collective-permute-start | bytes 393224 | tf_op jit(solution)/shard_map/ppermute | solution.py:25
  132.4 2.4 %collective-permute-done.7 = bf16[128,512]{1,0:T(8,128)(2,1)S(1)} collective-permute-done((bf16[128,512]{1,0:T(8,128)(2,1)S(1)}, bf16[128,512]{1,0:T(8,128)(2,1)S(1)}, u32[]{:S(2)}, u32[]{:S(2)}) %collective-permute-start.7) | collective-permute-done | bytes 131104 | tf_op jit(solution)/shard_map/ppermute | solution.py:25
  134.8 4.8 %collective-permute-done.9 = bf16[128,512]{1,0:T(8,128)(2,1)S(1)} collective-permute-done((bf16[128,512]{1,0:T(8,128)(2,1)S(1)}, bf16[128,512]{1,0:T(8,128)(2,1)S(1)}, u32[]{:S(2)}, u32[]{:S(2)}) %collective-permute-start.9) | collective-permute-done | bytes 131104 | tf_op jit(solution)/shard_map/ppermute | solution.py:25
  139.7 5.4 %collective-permute-done.8 = bf16[128,512]{1,0:T(8,128)(2,1)S(1)} collective-permute-done((bf16[128,512]{1,0:T(8,128)(2,1)S(1)}, bf16[128,512]{1,0:T(8,128)(2,1)S(1)}, u32[]{:S(2)}, u32[]{:S(2)}) %collective-permute-start.8) | collective-permute-done | bytes 131104 | tf_op jit(solution)/shard_map/ppermute | solution.py:25
  145.1 0.8 add_convert_fusion
  (53 shorter events, 1.9 us)
Async XLA Ops:
  1.6 10.9 %collective-permute-start.1 = (bf16[136,512]{1,0:T(8,128)(2,1)S(1)}, bf16[136,512]{1,0:T(8,128)(2,1)S(1)}, u32[]{:S(2)}, u32[]{:S(2)}) collective-permute-start(bf16[136,512]{1,0:T(8,128)(2,1)S(1)} %fusion.12.refs_0_), channel_id=1, source_target_pairs={{0,4},{1,5},{2,6},{3,7},{4,0},{5,1},{6,2},{7,3},{8,12},{9,13},{10,... | collective-permute-start | bytes 417800 | tf_op jit(solution)/shard_map/ppermute | solution.py:25
  5.7 9.4 %collective-permute-start = (bf16[136,512]{1,0:T(8,128)(2,1)S(1)}, bf16[136,512]{1,0:T(8,128)(2,1)S(1)}, u32[]{:S(2)}, u32[]{:S(2)}) collective-permute-start(bf16[136,512]{1,0:T(8,128)(2,1)S(1)} %fusion.12.refs_0_), channel_id=1, source_target_pairs={{0,2},{1,3},{2,0},{3,1},{4,6},{5,7},{6,4},{7,5},{8,10},{9,11},{10,... | collective-permute-start | bytes 417800 | tf_op jit(solution)/shard_map/ppermute | solution.py:25
  12.5 5.1 %collective-permute-start.2 = (bf16[136,512]{1,0:T(8,128)(2,1)S(1)}, bf16[136,512]{1,0:T(8,128)(2,1)S(1)}, u32[]{:S(2)}, u32[]{:S(2)}) collective-permute-start(bf16[136,512]{1,0:T(8,128)(2,1)S(1)} %collective-permute-done.1.refs_2_), channel_id=1, source_target_pairs={{0,2},{1,3},{2,0},{3,1},{4,6},{5,7},{6,4},{7,5},{8,10},{9,11},{10,... | collective-permute-start | bytes 417800 | tf_op jit(solution)/shard_map/ppermute | solution.py:25
  13.1 6.5 %collective-permute-start.10 = (bf16[136,512]{1,0:T(8,128)(2,1)S(1)}, bf16[136,512]{1,0:T(8,128)(2,1)S(1)}, u32[]{:S(2)}, u32[]{:S(2)}) collective-permute-start(bf16[136,512]{1,0:T(8,128)(2,1)S(1)} %fusion.12.refs_0_), channel_id=1, source_target_pairs={{0,1},{1,0},{2,3},{3,2},{4,5},{5,4},{6,7},{7,6},{8,9},{9,8},{10,11... | collective-permute-start | bytes 417800 | tf_op jit(solution)/shard_map/ppermute | solution.py:25
  14.6 8.0 %collective-permute-start.12 = (bf16[136,512]{1,0:T(8,128)(2,1)S(1)}, bf16[136,512]{1,0:T(8,128)(2,1)S(1)}, u32[]{:S(2)}, u32[]{:S(2)}) collective-permute-start(bf16[136,512]{1,0:T(8,128)(2,1)S(1)} %collective-permute-done.1.refs_2_), channel_id=1, source_target_pairs={{0,1},{1,0},{2,3},{3,2},{4,5},{5,4},{6,7},{7,6},{8,9},{9,8},{10,11... | collective-permute-start | bytes 417800 | tf_op jit(solution)/shard_map/ppermute | solution.py:25
  15.1 10.5 %collective-permute-start.11 = (bf16[136,512]{1,0:T(8,128)(2,1)S(1)}, bf16[136,512]{1,0:T(8,128)(2,1)S(1)}, u32[]{:S(2)}, u32[]{:S(2)}) collective-permute-start(bf16[136,512]{1,0:T(8,128)(2,1)S(1)} %collective-permute-done.refs_1_), channel_id=1, source_target_pairs={{0,1},{1,0},{2,3},{3,2},{4,5},{5,4},{6,7},{7,6},{8,9},{9,8},{10,11... | collective-permute-start | bytes 417800 | tf_op jit(solution)/shard_map/ppermute | solution.py:25
  17.6 9.8 %collective-permute-start.13 = (bf16[136,512]{1,0:T(8,128)(2,1)S(1)}, bf16[136,512]{1,0:T(8,128)(2,1)S(1)}, u32[]{:S(2)}, u32[]{:S(2)}) collective-permute-start(bf16[136,512]{1,0:T(8,128)(2,1)S(1)} %collective-permute-done.2.refs_3_), channel_id=1, source_target_pairs={{0,1},{1,0},{2,3},{3,2},{4,5},{5,4},{6,7},{7,6},{8,9},{9,8},{10,11... | collective-permute-start | bytes 417800 | tf_op jit(solution)/shard_map/ppermute | solution.py:25
  19.2 22.2 %copy-start.8 = (s32[2]{0:T(128)}, s32[2]{0:T(128)S(1)}, u32[]{:S(2)}) copy-start(s32[2]{0:T(128)S(1)} %pad_add_fusion.place) | copy-start | bytes 28
  27.4 0.9 copy-start.2
  28.3 13.1 %copy-start.3 = (bf16[512,128]{1,0:T(8,128)(2,1)S(1)}, bf16[512,128]{1,0:T(8,128)(2,1)}, u32[]{:S(2)}) copy-start(bf16[512,128]{1,0:T(8,128)(2,1)} %refs_4_.3) | copy-start | bytes 393220
  38.8 0.9 copy-start.1
  39.7 0.6 copy-start.5
  40.3 0.6 copy-start.7
  40.9 0.5 copy-start.10
  41.4 11.3 %collective-permute-start.14 = (bf16[2,1040,384]{2,1,0:T(8,128)(2,1)S(1)}, bf16[2,1040,384]{2,1,0:T(8,128)(2,1)S(1)}, u32[]{:S(2)}, u32[]{:S(2)}) collective-permute-start(bf16[2,1040,384]{2,1,0:T(8,128)(2,1)S(1)} %get-tuple-element.36), channel_id=1, source_target_pairs={{0,8},{8,0},{16,24},{24,16},{1,9},{9,1},{17,25},{25,17},{2,10},{10... | collective-permute-start | bytes 4792328 | tf_op jit(solution)/shard_map/ppermute | solution.py:25
  52.0 3.9 %copy-start = (bf16[1040,384]{1,0:T(8,128)(2,1)}, bf16[1040,384]{1,0:T(8,128)(2,1)S(1)}, u32[]{:S(2)}) copy-start(bf16[1040,384]{1,0:T(8,128)(2,1)S(1)} %get-tuple-element.26.near) | copy-start | bytes 2396164
  52.1 3.9 %copy-start.4 = (s32[16,512]{1,0:T(8,128)}, s32[16,512]{1,0:T(8,128)S(1)}, u32[]{:S(2)}) copy-start(s32[16,512]{1,0:T(8,128)S(1)} %get-tuple-element.25.pos) | copy-start | bytes 98308
  52.1 3.9 %copy-start.6 = (s32[32,128]{1,0:T(8,128)}, s32[32,128]{1,0:T(8,128)S(1)}, u32[]{:S(2)}) copy-start(s32[32,128]{1,0:T(8,128)S(1)} %get-tuple-element.24.ids) | copy-start | bytes 49156
  52.1 3.9 %copy-start.9 = (s32[16]{0:T(128)}, s32[16]{0:T(128)S(1)}, u32[]{:S(2)}) copy-start(s32[16]{0:T(128)S(1)} %get-tuple-element.23.meta) | copy-start | bytes 196
  52.1 3.6 %collective-permute-start.3 = (bf16[2,1040,384]{2,1,0:T(8,128)(2,1)S(1)}, bf16[2,1040,384]{2,1,0:T(8,128)(2,1)S(1)}, u32[]{:S(2)}, u32[]{:S(2)}) collective-permute-start(bf16[2,1040,384]{2,1,0:T(8,128)(2,1)S(1)} %get-tuple-element.27), channel_id=1, source_target_pairs={{0,8},{8,0},{16,24},{24,16},{1,9},{9,1},{17,25},{25,17},{2,10},{10... | collective-permute-start | bytes 4792328 | tf_op jit(solution)/shard_map/ppermute | solution.py:25
  52.7 3.3 %copy-start.12 = (bf16[2,1040,384]{2,1,0:T(8,128)(2,1)}, bf16[2,1040,384]{2,1,0:T(8,128)(2,1)S(1)}, u32[]{:S(2)}) copy-start(bf16[2,1040,384]{2,1,0:T(8,128)(2,1)S(1)} %collective-permute-done.14.beside) | copy-start | bytes 4792324
  52.9 20.7 %collective-permute-start.15 = (bf16[1040,384]{1,0:T(8,128)(2,1)S(1)}, bf16[1040,384]{1,0:T(8,128)(2,1)S(1)}, u32[]{:S(2)}, u32[]{:S(2)}) collective-permute-start(bf16[1040,384]{1,0:T(8,128)(2,1)S(1)} %fusion), channel_id=1, source_target_pairs={{0,16},{8,24},{16,0},{24,8},{1,17},{9,25},{17,1},{25,9},{2,18},{10... | collective-permute-start | bytes 2396168 | tf_op jit(solution)/shard_map/ppermute | solution.py:25
  55.7 29.4 %copy-start.11 = (bf16[2,1040,384]{2,1,0:T(8,128)(2,1)}, bf16[2,1040,384]{2,1,0:T(8,128)(2,1)S(1)}, u32[]{:S(2)}) copy-start(bf16[2,1040,384]{2,1,0:T(8,128)(2,1)S(1)} %collective-permute-done.3.beside) | copy-start | bytes 4792324
  56.0 33.8 %collective-permute-start.4 = (bf16[1040,384]{1,0:T(8,128)(2,1)S(1)}, bf16[1040,384]{1,0:T(8,128)(2,1)S(1)}, u32[]{:S(2)}, u32[]{:S(2)}) collective-permute-start(bf16[1040,384]{1,0:T(8,128)(2,1)S(1)} %fusion.1), channel_id=1, source_target_pairs={{0,16},{8,24},{16,0},{24,8},{1,17},{9,25},{17,1},{25,9},{2,18},{10... | collective-permute-start | bytes 2396168 | tf_op jit(solution)/shard_map/ppermute | solution.py:25
  73.6 0.9 copy-start.14
  85.2 16.3 %collective-permute-start.16 = (bf16[2,512,512]{2,1,0:T(8,128)(2,1)}, bf16[2,512,512]{2,1,0:T(8,128)(2,1)S(1)}, u32[]{:S(2)}, u32[]{:S(2)}) collective-permute-start(bf16[2,512,512]{2,1,0:T(8,128)(2,1)} %get-tuple-element.39), channel_id=1, source_target_pairs={{0,8},{8,0},{16,24},{24,16},{1,9},{9,1},{17,25},{25,17},{2,10},{10... | collective-permute-start | bytes 3145736 | tf_op jit(solution)/shard_map/ppermute | solution.py:25
  89.8 0.9 copy-start.13
  90.7 10.8 %copy-start.15 = (bf16[512,512]{1,0:T(8,128)(2,1)S(1)}, bf16[512,512]{1,0:T(8,128)(2,1)}, u32[]{:S(2)}) copy-start(bf16[512,512]{1,0:T(8,128)(2,1)} %get-tuple-element.40) | copy-start | bytes 1572868
  101.4 3.0 %copy-start.16 = (bf16[512,512]{1,0:T(8,128)(2,1)S(1)}, bf16[512,512]{1,0:T(8,128)(2,1)}, u32[]{:S(2)}) copy-start(bf16[512,512]{1,0:T(8,128)(2,1)} %get-tuple-element.31) | copy-start | bytes 1572868
  101.4 15.1 %copy-start.18 = (bf16[512,512]{1,0:T(8,128)(2,1)S(1)}, bf16[512,512]{1,0:T(8,128)(2,1)}, u32[]{:S(2)}) copy-start(bf16[512,512]{1,0:T(8,128)(2,1)} %get-tuple-element.38) | copy-start | bytes 1572868
  101.4 2.9 %collective-permute-start.5 = (bf16[2,512,512]{2,1,0:T(8,128)(2,1)}, bf16[2,512,512]{2,1,0:T(8,128)(2,1)S(1)}, u32[]{:S(2)}, u32[]{:S(2)}) collective-permute-start(bf16[2,512,512]{2,1,0:T(8,128)(2,1)} %get-tuple-element.30), channel_id=1, source_target_pairs={{0,8},{8,0},{16,24},{24,16},{1,9},{9,1},{17,25},{25,17},{2,10},{10... | collective-permute-start | bytes 3145736 | tf_op jit(solution)/shard_map/ppermute | solution.py:25
  101.7 9.2 %collective-permute-start.17 = (bf16[256,512]{1,0:T(8,128)(2,1)S(1)}, bf16[256,512]{1,0:T(8,128)(2,1)S(1)}, u32[]{:S(2)}, u32[]{:S(2)}) collective-permute-start(bf16[256,512]{1,0:T(8,128)(2,1)S(1)} %get-tuple-element.43), channel_id=1, source_target_pairs={{0,16},{8,24},{16,0},{24,8},{1,17},{9,25},{17,1},{25,9},{2,18},{10... | collective-permute-start | bytes 786440 | tf_op jit(solution)/shard_map/ppermute | solution.py:25
  103.2 13.3 %collective-permute-start.20 = (bf16[256,512]{1,0:T(8,128)(2,1)S(1)}, bf16[256,512]{1,0:T(8,128)(2,1)S(1)}, u32[]{:S(2)}, u32[]{:S(2)}) collective-permute-start(bf16[256,512]{1,0:T(8,128)(2,1)S(1)} %get-tuple-element.44), channel_id=1, source_target_pairs={{0,16},{8,24},{16,0},{24,8},{1,17},{9,25},{17,1},{25,9},{2,18},{10... | collective-permute-start | bytes 786440 | tf_op jit(solution)/shard_map/ppermute | solution.py:25
  104.5 22.8 %copy-start.17 = (bf16[512,512]{1,0:T(8,128)(2,1)S(1)}, bf16[512,512]{1,0:T(8,128)(2,1)}, u32[]{:S(2)}) copy-start(bf16[512,512]{1,0:T(8,128)(2,1)} %get-tuple-element.29) | copy-start | bytes 1572868
  104.5 22.8 %collective-permute-start.6 = (bf16[512,512]{1,0:T(8,128)(2,1)S(1)}, bf16[512,512]{1,0:T(8,128)(2,1)S(1)}, u32[]{:S(2)}, u32[]{:S(2)}) collective-permute-start(bf16[512,512]{1,0:T(8,128)(2,1)S(1)} %fusion.2), channel_id=1, source_target_pairs={{0,16},{8,24},{16,0},{24,8},{1,17},{9,25},{17,1},{25,9},{2,18},{10... | collective-permute-start | bytes 1572872 | tf_op jit(solution)/shard_map/ppermute | solution.py:25
  116.8 11.3 %collective-permute-start.18 = (bf16[128,512]{1,0:T(8,128)(2,1)S(1)}, bf16[128,512]{1,0:T(8,128)(2,1)S(1)}, u32[]{:S(2)}, u32[]{:S(2)}) collective-permute-start(bf16[128,512]{1,0:T(8,128)(2,1)S(1)} %get-tuple-element.48), channel_id=1, source_target_pairs={{0,1},{1,0},{2,3},{3,2},{4,5},{5,4},{6,7},{7,6},{8,9},{9,8},{10,11... | collective-permute-start | bytes 393224 | tf_op jit(solution)/shard_map/ppermute | solution.py:25
  118.3 14.1 %collective-permute-start.19 = (bf16[128,512]{1,0:T(8,128)(2,1)S(1)}, bf16[128,512]{1,0:T(8,128)(2,1)S(1)}, u32[]{:S(2)}, u32[]{:S(2)}) collective-permute-start(bf16[128,512]{1,0:T(8,128)(2,1)S(1)} %get-tuple-element.49), channel_id=1, source_target_pairs={{0,3},{1,2},{2,1},{3,0},{4,7},{5,6},{6,5},{7,4},{8,11},{9,10},{10,... | collective-permute-start | bytes 393224 | tf_op jit(solution)/shard_map/ppermute | solution.py:25
  118.8 13.6 %collective-permute-start.21 = (bf16[128,512]{1,0:T(8,128)(2,1)S(1)}, bf16[128,512]{1,0:T(8,128)(2,1)S(1)}, u32[]{:S(2)}, u32[]{:S(2)}) collective-permute-start(bf16[128,512]{1,0:T(8,128)(2,1)S(1)} %get-tuple-element.50), channel_id=1, source_target_pairs={{0,5},{1,4},{2,7},{3,6},{4,1},{5,0},{6,3},{7,2},{8,13},{9,12},{10,... | collective-permute-start | bytes 393224 | tf_op jit(solution)/shard_map/ppermute | solution.py:25
  122.9 9.5 %collective-permute-start.22 = (bf16[128,512]{1,0:T(8,128)(2,1)S(1)}, bf16[128,512]{1,0:T(8,128)(2,1)S(1)}, u32[]{:S(2)}, u32[]{:S(2)}) collective-permute-start(bf16[128,512]{1,0:T(8,128)(2,1)S(1)} %get-tuple-element.51), channel_id=1, source_target_pairs={{0,7},{1,6},{2,5},{3,4},{4,3},{5,2},{6,1},{7,0},{8,15},{9,14},{10,... | collective-permute-start | bytes 393224 | tf_op jit(solution)/shard_map/ppermute | solution.py:25
  127.5 7.3 %collective-permute-start.7 = (bf16[128,512]{1,0:T(8,128)(2,1)S(1)}, bf16[128,512]{1,0:T(8,128)(2,1)S(1)}, u32[]{:S(2)}, u32[]{:S(2)}) collective-permute-start(bf16[128,512]{1,0:T(8,128)(2,1)S(1)} %get-tuple-element.45), channel_id=1, source_target_pairs={{0,2},{1,3},{2,0},{3,1},{4,6},{5,7},{6,4},{7,5},{8,10},{9,11},{10,... | collective-permute-start | bytes 393224 | tf_op jit(solution)/shard_map/ppermute | solution.py:25
  128.0 11.6 %collective-permute-start.9 = (bf16[128,512]{1,0:T(8,128)(2,1)S(1)}, bf16[128,512]{1,0:T(8,128)(2,1)S(1)}, u32[]{:S(2)}, u32[]{:S(2)}) collective-permute-start(bf16[128,512]{1,0:T(8,128)(2,1)S(1)} %get-tuple-element.46), channel_id=1, source_target_pairs={{0,6},{1,7},{2,4},{3,5},{4,2},{5,3},{6,0},{7,1},{8,14},{9,15},{10,... | collective-permute-start | bytes 393224 | tf_op jit(solution)/shard_map/ppermute | solution.py:25
  132.4 12.6 %collective-permute-start.8 = (bf16[128,512]{1,0:T(8,128)(2,1)S(1)}, bf16[128,512]{1,0:T(8,128)(2,1)S(1)}, u32[]{:S(2)}, u32[]{:S(2)}) collective-permute-start(bf16[128,512]{1,0:T(8,128)(2,1)S(1)} %get-tuple-element.47), channel_id=1, source_target_pairs={{0,4},{1,5},{2,6},{3,7},{4,0},{5,1},{6,2},{7,3},{8,12},{9,13},{10,... | collective-permute-start | bytes 393224 | tf_op jit(solution)/shard_map/ppermute | solution.py:25
